TPU v7x, 32 devices: a whole 2x2x4 slice. The times are simulated.
32 devices in a mesh: groups: 2 (over y), ctx: 4 (over z), ch: 4 (over x, core).
Axes of the slice: x: 2, y: 2, z: 4, core: 2. Of those that a mesh axis runs over, the one named last changes fastest.
Arguments:
- projections: bfloat16 [1024, 3, 4096], P(('groups', 'ctx'), None, 'ch'), parts along dimension 0, may hold values from -6 to 6
- short_taps: float32 [3, 3, 4096], P(None, None, 'ch'), may hold values from -3 to 3
- residues: float32 [4096, 16], P(('ch', 'ctx')), may hold values from -2 to 2
- decay_rates: float32 [4096, 16], P(('ch', 'ctx')), may hold values from 0.25 to 16
- skip_gain: float32 [4096], P(('ch', 'ctx')), may hold values from -3 to 3
- grad_mixed: bfloat16 [1024, 2048], P(('groups', 'ctx'), 'ch'), parts along dimension 0, may hold values from -6 to 6
- out_weight: bfloat16 [4096, 2048], P('ch', 'ctx'), may hold values from -0.09375 to 0.09375
Outputs:
- grad_projections: bfloat16 [1024, 3, 4096], P(('groups', 'ctx'), None, 'ch'), parts along dimension 0
- grad_short: float32 [6, 3, 4096], P('groups', None, 'ch'), parts along dimension 0
- grad_skip: float32 [8192], P(('groups', 'ch', 'ctx')), parts along dimension 0
- grad_residues: float32 [8192, 16], P(('groups', 'ch', 'ctx')), parts along dimension 0
- grad_log_rates: float32 [8192, 16], P(('groups', 'ch', 'ctx')), parts along dimension 0
- grad_weight: float32 [8192, 2048], P(('groups', 'ch'), 'ctx'), parts along dimension 0
There are 2 independent parts, one for each index of `groups`. A program takes and returns all parts, laid end to end along the dimension named above; an argument that names none is the same for every part. Nothing has to cross between parts.
All inputs are finite; a program needn't handle non-finite values.
Results may differ from a plain program's by a relative error of at most 0.006.
Values may be sent and summed in bfloat16 or wider, within the bound.
A program may use at most 64 MiB of HBM per device.

v0:
```python
from functools import partial
import math

import jax
import jax.numpy as jnp
from jax import lax
from jax.sharding import PartitionSpec as P

SHORT = 3


def from_behind(x, axis, by):
    peers = lax.axis_size(axis)
    pairs = [(i, i + by) for i in range(peers) if 0 <= i + by < peers]
    return lax.ppermute(x, axis, pairs)


def make_filter(residues, decay_rates, seq_len):
    positions = jnp.arange(seq_len, dtype=jnp.float32) / seq_len
    amplitude = residues * jnp.sqrt(2.0 * decay_rates / seq_len)
    basis = jnp.exp(-decay_rates[:, :, None] * positions[None, None, :])
    return jnp.einsum("cn,cnt->ct", amplitude, basis, precision=lax.Precision.HIGHEST)


def circle(rows_count, cols_count, period):
    left_idx = jnp.arange(rows_count, dtype=jnp.int32)[:, None]
    right_idx = jnp.arange(cols_count, dtype=jnp.int32)[None, :]
    angle = (left_idx * right_idx % period).astype(jnp.float32) * (2.0 * math.pi / period)
    return (jnp.cos(angle), jnp.sin(angle))


def spectral_tables(length):
    factor_a = 1
    while factor_a * factor_a * 4 <= length and length % (factor_a * 2) == 0:
        factor_a = factor_a * 2
    factor_b = length // factor_a
    a_cos, a_sin = circle(factor_a, factor_a, factor_a)
    b_cos, b_sin = circle(factor_b, factor_b, factor_b)
    t_cos, t_sin = circle(factor_a, factor_b, length)
    return (length, factor_a, factor_b, a_cos, a_sin, b_cos, b_sin, t_cos, t_sin)


def forward_dft(signal, tables):
    length, factor_a, factor_b, a_cos, a_sin, b_cos, b_sin, t_cos, t_sin = tables
    highest = lax.Precision.HIGHEST
    channels, seq_len = signal.shape
    grid = jnp.pad(signal, ((0, 0), (0, length - seq_len))).reshape(channels, factor_a, factor_b)
    part_real = jnp.einsum("ka,cab->ckb", a_cos, grid, precision=highest)
    part_imag = -jnp.einsum("ka,cab->ckb", a_sin, grid, precision=highest)
    turn_real = part_real * t_cos + part_imag * t_sin
    turn_imag = part_imag * t_cos - part_real * t_sin
    out_real = jnp.einsum("ckb,bm->ckm", turn_real, b_cos, precision=highest) + jnp.einsum(
        "ckb,bm->ckm", turn_imag, b_sin, precision=highest
    )
    out_imag = jnp.einsum("ckb,bm->ckm", turn_imag, b_cos, precision=highest) - jnp.einsum(
        "ckb,bm->ckm", turn_real, b_sin, precision=highest
    )
    return (out_real, out_imag)


def inverse_dft(spec_real, spec_imag, seq_len, tables):
    length, factor_a, factor_b, a_cos, a_sin, b_cos, b_sin, t_cos, t_sin = tables
    highest = lax.Precision.HIGHEST
    channels = spec_real.shape[0]
    mid_real = jnp.einsum("ckm,mb->ckb", spec_real, b_cos, precision=highest) - jnp.einsum(
        "ckm,mb->ckb", spec_imag, b_sin, precision=highest
    )
    mid_imag = jnp.einsum("ckm,mb->ckb", spec_imag, b_cos, precision=highest) + jnp.einsum(
        "ckm,mb->ckb", spec_real, b_sin, precision=highest
    )
    turn_real = mid_real * t_cos - mid_imag * t_sin
    turn_imag = mid_imag * t_cos + mid_real * t_sin
    values = jnp.einsum("ak,ckb->cab", a_cos, turn_real, precision=highest) - jnp.einsum(
        "ak,ckb->cab", a_sin, turn_imag, precision=highest
    )
    return values.reshape(channels, length)[:, :seq_len] / length


def short_mix(extended, short_taps, tokens):
    running = jnp.zeros((tokens,) + extended.shape[1:], jnp.float32)
    for lag_index in range(SHORT):
        start_row = SHORT - 1 - lag_index
        running = running + short_taps[lag_index] * extended[start_row : start_row + tokens]
    return running


def mix_long(gate_cols, spec_h, gain, seq_len, tables):
    gate_f = gate_cols.astype(jnp.float32)
    u_real, u_imag = forward_dft(gate_f, tables)
    prod_real = spec_h[0] * u_real - spec_h[1] * u_imag
    prod_imag = spec_h[0] * u_imag + spec_h[1] * u_real
    mix_cols = (inverse_dft(prod_real, prod_imag, seq_len, tables) + gain[:, None] * gate_f).astype(
        jnp.bfloat16
    )
    return (mix_cols, (u_real, u_imag))


def grad_long(grad_cols_in, gate_cols, spec_u, spec_h, gain, seq_len, tables):
    grad_f = grad_cols_in.astype(jnp.float32)
    g_real, g_imag = forward_dft(grad_f, tables)
    back_real = spec_h[0] * g_real + spec_h[1] * g_imag
    back_imag = spec_h[0] * g_imag - spec_h[1] * g_real
    grad_cols = (
        inverse_dft(back_real, back_imag, seq_len, tables) + gain[:, None] * grad_f
    ).astype(jnp.bfloat16)
    corr_real = g_real * spec_u[0] + g_imag * spec_u[1]
    corr_imag = g_imag * spec_u[0] - g_real * spec_u[1]
    grad_filter = inverse_dft(corr_real, corr_imag, seq_len, tables)
    skip_sum = jnp.sum(grad_f * gate_cols.astype(jnp.float32), axis=1)
    return (grad_cols, grad_filter, skip_sum)


def body(projections, short_taps, residues, decay_rates, skip_gain, grad_mixed, out_weight):
    tokens = projections.shape[0]
    seq_len = tokens * lax.axis_size("ctx")
    norm_factor = math.sqrt(seq_len)
    tables = spectral_tables(2 * seq_len)
    earlier = from_behind(projections[tokens - SHORT + 1 :], "ctx", 1)
    ext_proj = jnp.concatenate([earlier, projections], axis=0)
    mixed_in = short_mix(ext_proj, short_taps, tokens)
    query_rows = mixed_in[:, 0]
    key_rows = mixed_in[:, 1]
    value_rows = mixed_in[:, 2]
    gated_rows = (key_rows * value_rows).astype(jnp.bfloat16)
    long_filter, filter_vjp = jax.vjp(partial(make_filter, seq_len=seq_len), residues, decay_rates)
    spec_h = forward_dft(long_filter, tables)
    out_rows = lax.all_gather(grad_mixed, "ch", axis=1, tiled=True)
    grad_out = lax.dot_general(
        out_rows,
        lax.all_gather(out_weight, "ctx", axis=1, tiled=True),
        (((1,), (1,)), ((), ())),
        preferred_element_type=jnp.float32,
    )
    grad_y = (grad_out * query_rows).astype(jnp.bfloat16)
    gate_cols, grad_cols_in = (
        lax.all_to_all(gated_rows.T, "ctx", split_axis=0, concat_axis=1, tiled=True),
        lax.all_to_all(grad_y.T, "ctx", split_axis=0, concat_axis=1, tiled=True),
    )
    mix_cols, spec_u = mix_long(gate_cols, spec_h, skip_gain, seq_len, tables)
    grad_cols, grad_filter, skip_sum = grad_long(
        grad_cols_in, gate_cols, spec_u, spec_h, skip_gain, seq_len, tables
    )
    returned = (
        lax.all_to_all(mix_cols, "ctx", split_axis=1, concat_axis=0, tiled=True),
        lax.all_to_all(grad_cols, "ctx", split_axis=1, concat_axis=0, tiled=True),
    )
    mix_rows = returned[0].T
    grad_gated = returned[1].T
    grad_res, grad_rate = filter_vjp(grad_filter)
    grad_residues = grad_res / norm_factor
    grad_log_rates = grad_rate * decay_rates / norm_factor
    grad_skip = skip_sum / norm_factor
    mixed_out = (query_rows * mix_rows).astype(jnp.bfloat16)
    grad_mix = jnp.stack(
        [grad_out * mix_rows, grad_gated * value_rows, grad_gated * key_rows], axis=1
    )
    later = from_behind(grad_mix[: SHORT - 1], "ctx", -1)
    ext_grad = jnp.concatenate([grad_mix, later], axis=0)
    running = jnp.zeros(grad_mix.shape, jnp.float32)
    short_terms = []
    for lag_index in range(SHORT):
        running = running + short_taps[lag_index] * ext_grad[lag_index : lag_index + tokens]
        start_row = SHORT - 1 - lag_index
        short_terms.append(jnp.sum(grad_mix * ext_proj[start_row : start_row + tokens], axis=0))
    grad_projections = running.astype(jnp.bfloat16)
    grad_short = lax.psum(jnp.stack(short_terms, axis=0), "ctx") / norm_factor
    partial_term = lax.dot_general(
        mixed_out, out_rows, (((0,), (0,)), ((), ())), preferred_element_type=jnp.float32
    )
    weight_sum = lax.psum_scatter(partial_term, "ctx", scatter_dimension=1, tiled=True)
    grad_weight = weight_sum / norm_factor
    return (grad_projections, grad_short, grad_skip, grad_residues, grad_log_rates, grad_weight)


def solution(mesh):
    return jax.shard_map(
        body,
        mesh=mesh,
        in_specs=(
            P(("groups", "ctx"), None, "ch"),
            P(None, None, "ch"),
            P(("ch", "ctx"), None),
            P(("ch", "ctx"), None),
            P(("ch", "ctx")),
            P(("groups", "ctx"), "ch"),
            P("ch", "ctx"),
        ),
        out_specs=(
            P(("groups", "ctx"), None, "ch"),
            P("groups", None, "ch"),
            P(("groups", "ch", "ctx")),
            P(("groups", "ch", "ctx"), None),
            P(("groups", "ch", "ctx"), None),
            P(("groups", "ch"), "ctx"),
        ),
        check_vma=False,
    )
```

profile of v0, /device:TPU:0, one launch (start us, length us, event | category | flops | bytes accessed | tf_op | source)
XLA Modules:
  0.0 377.9 jit_solution(4330585628768449797)
XLA Ops:
  7.9 0.8 slice.52
  8.7 4.9 %collective-permute-start = (bf16[2,3,1024]{2,0,1:T(2,128)(2,1)S(1)}, bf16[2,3,1024]{2,0,1:T(2,128)(2,1)S(1)}, u32[]{:S(2)}, u32[]{:S(2)}) collective-permute-start(bf16[2,3,1024]{2,0,1:T(2,128)(2,1)S(1)} %slice.52), channel_id=1, source_target_pairs={{0,4},{4,8},{8,12},{1,5},{5,9},{9,13},{2,6},{6,10},{10,14},{3,7},{... | collective-permute-start | bytes 36872 | tf_op jit(solution)/shard_map/ppermute | solution.py:15
  13.7 7.4 %all_gather.6 = bf16[128,2048]{1,0:T(8,128)(2,1)S(1)} all-gather(bf16[128,512]{1,0:T(8,128)(2,1)} %param.12), channel_id=1, replica_groups=mesh['groups'=2,'ctx'=4,'ch'=4] {'ch'}, dimensions={1}, use_global_device_ids=true | all-gather | bytes 655360 | tf_op jit(solution)/shard_map/all_gather | solution.py:127
  21.7 71.3 %all-gather.2.cloned.1.call-done = bf16[1024,2048]{1,0:T(8,128)(2,1)} async-done(((bf16[1024,512]{1,0:T(8,128)(2,1)}), bf16[1024,2048]{1,0:T(8,128)(2,1)}) %all-gather.2.cloned.1.call-update) | async-done | bytes 4194320 | tf_op jit(solution)/shard_map/all_gather | solution.py:130
  93.1 4.5 %multiply_convert_fusion.1 = (bf16[128,1024]{1,0:T(8,128)(2,1)S(1)}, bf16[128,1024]{1,0:T(8,128)(2,1)S(1)}, f32[128,1024]{1,0:T(8,128)}) fusion(f32[128,3,1024]{2,0,1:T(8,128)S(1)} %fusion.1, bf16[128,2048]{1,0:T(8,128)(2,1)S(1)} %all_gather.6, bf16[1024,2048]{1,0:T(8,128)(2,1)} %all-gather.2.cloned.1.call-done), kind=kOutput, calls=%fused_computation.133 | convolution fusion | flops 537395200 | bytes 7340032 | tf_op jit(solution)/shard_map/dot_general | solution.py:128
  98.3 3.4 all-to-all-start.2
  104.3 6.7 %all-to-all-done.2 = bf16[4,256,128]{1,2,0:T(8,128)(2,1)S(1)} async-done(((bf16[4,256,128]{1,2,0:T(8,128)(2,1)}), bf16[4,256,128]{1,2,0:T(8,128)(2,1)S(1)}, u32[]{:S(2)}, u32[]{:S(2)}) %all-to-all-start.2) | async-done | bytes 262176 | tf_op jit(solution)/shard_map/all_to_all | solution.py:137
  110.9 3.4 all-to-all-start
  114.7 2.7 fusion.10
  117.4 2.7 convolution_bitcast_fusion
  120.1 1.2 all-to-all-done
  121.4 1.7 convolution_bitcast_fusion.1
  123.1 2.1 multiply_add_fusion.4
  125.3 1.7 fusion.43
  127.0 1.7 fusion.47
  128.7 2.0 convolution_subtract_fusion.4
  130.7 1.7 fusion.39
  132.5 1.7 fusion.35
  134.2 1.8 convolution_add_fusion
  136.0 1.8 convolution_add_fusion.1
  137.9 3.1 multiply_add_fusion
  141.0 1.1 fusion.112
  142.1 1.1 fusion.86
  143.2 1.5 fusion.88
  144.8 1.1 fusion.110
  145.9 3.7 fusion.17
  149.6 3.7 fusion.8
  153.9 0.9 slice_multiply_fusion.2
  154.7 2.0 copy.328
  156.8 6.3 %multiply_reduce_fusion.2 = (f32[256,16]{1,0:T(8,128)}, f32[256,512]{1,0:T(8,128)}) fusion(f32[256,16]{1,0:T(8,128)} %copy.327, f32[256,512]{1,0:T(8,128)} %copy.328, f32[512]{0:T(512)S(1)} %iota_multiply_fusion.1, f32[256,16]{1,0:T(8,128)} %copy.203), kind=kLoop, calls=%fused_computation.2 | loop fusion | flops 14544896 | bytes 1099776 | tf_op jit(solution)/shard_map/transpose(jvp())/reduce_sum | solution.py:21
  163.1 2.1 copy.273
  165.1 1.1 pad.10
  166.2 1.7 convolution_bitcast_fusion.2
  168.0 2.0 multiply_add_fusion.5
  170.0 1.7 fusion.55
  171.7 1.7 fusion.51
  173.5 1.8 convolution_add_fusion.2
  175.4 2.4 multiply_subtract_fusion.3
  177.8 1.3 fusion.122
  179.2 1.1 fusion.96
  180.3 1.1 fusion.98
  181.4 1.1 fusion.120
  182.5 1.1 fusion.116
  183.6 1.1 fusion.90
  184.7 1.1 fusion.92
  185.8 1.1 fusion.114
  186.9 3.7 fusion.31
  190.6 4.1 %fusion.11 = f32[256,32,32]{0,1,2:T(8,128)S(1)} fusion(f32[256,32,32]{0,2,1:T(8,128)S(1)} %fusion.31, f32[32,32]{0,1:T(8,128)S(1)} %copy.207, f32[32,32]{0,1:T(8,128)S(1)} %copy.205, f32[256,32,32]{0,2,1:T(8,128)S(1)} %fusion.98, f32[256,32,32]{0,2,1:T(8,128)S(1)} %fusion.122, f32[256,32,32]{0,2,1:T(8,128)S(1)} %fusion.96, f32[256,32,32]{0,2,1:T(8,128)S(1)} %fusion.120), kind=kOutput, calls=%fused_computation.32 | convolution fusion | flops 102250496 | bytes 6299648 | tf_op jit(solution)/shard_map/ak,ckb->cab/dot_general | solution.py:73
  195.3 3.7 fusion.24
  199.0 3.7 fusion.9
  202.7 0.8 copy.256
  203.7 0.9 fusion.63
  204.5 10.8 %all_to_all.52 = bf16[256,4,128]{0,2,1:T(8,128)(2,1)S(1)} all-to-all(bf16[256,4,128]{0,2,1:T(8,128)(2,1)S(1)} %bitcast.240), channel_id=1, replica_groups=mesh['groups'=2,'ctx'=4,'ch'=4] {'ctx'}, dimensions={1} | all-to-all | bytes 524288 | tf_op jit(solution)/shard_map/all_to_all | solution.py:144
  215.4 4.5 %fusion.80 = f32[1024,2048]{1,0:T(8,128)} fusion(bf16[128,2048]{1,0:T(8,128)(2,1)S(1)} %all_gather.6, f32[1024,128]{0,1:T(8,128)S(1)} %bitcast.230, f32[128,3,1024]{2,0,1:T(8,128)S(1)} %fusion.1), kind=kOutput, calls=%fused_computation.146 | convolution fusion | flops 537133056 | bytes 9961472 | tf_op jit(solution)/shard_map/dot_general | solution.py:167
  219.9 3.6 all-to-all-start.3
  223.5 3.7 multiply_reduce_fusion
  228.1 8.6 %all-to-all-done.3 = bf16[256,4,128]{0,2,1:T(8,128)(2,1)S(1)} async-done(((bf16[256,4,128]{0,2,1:T(8,128)(2,1)}), bf16[256,4,128]{0,2,1:T(8,128)(2,1)S(1)}, u32[]{:S(2)}, u32[]{:S(2)}) %all-to-all-start.3) | async-done | bytes 262176 | tf_op jit(solution)/shard_map/all_to_all | solution.py:145
  236.8 1.3 fusion.64
  238.2 1.3 collective-permute-start.1
  240.1 7.0 %collective-permute-done.1 = f32[2,3,1024]{2,0,1:T(2,128)S(1)} collective-permute-done((f32[2,3,1024]{2,0,1:T(2,128)S(1)}, f32[2,3,1024]{2,0,1:T(2,128)S(1)}, u32[]{:S(2)}, u32[]{:S(2)}) %collective-permute-start.1) | collective-permute-done | bytes 24608 | tf_op jit(solution)/shard_map/ppermute | solution.py:15
  247.3 2.0 fusion.3
  249.3 19.5 %psum.7 = f32[3,3,1024]{2,1,0:T(4,128)S(1)} all-reduce(f32[3,3,1024]{2,1,0:T(4,128)S(1)} %pad_maximum_fusion.3), channel_id=1, replica_groups=mesh['groups'=2,'ctx'=4,'ch'=4] {'ctx'}, use_global_device_ids=true, to_apply=%region_3.4 | all-reduce | flops 9216 | bytes 73728 | tf_op jit(solution)/shard_map/psum | solution.py:166
  269.5 98.2 %reduce-scatter.2.cloned.1.call-done = f32[1024,512]{1,0:T(8,128)} async-done(((f32[1024,2048]{1,0:T(8,128)}), f32[1024,512]{1,0:T(8,128)}) %reduce-scatter.2.cloned.1.call-update) | async-done | bytes 2097168 | tf_op jit(solution)/shard_map/reduce_scatter | solution.py:170
  367.7 3.2 broadcast_multiply_fusion
  (71 shorter events, 9.0 us)
Async XLA Ops:
  7.2 14.0 %copy-start.9 = (bf16[128,3,1024]{2,0,1:T(8,128)(2,1)S(1)}, bf16[128,3,1024]{2,0,1:T(8,128)(2,1)}, u32[]{:S(2)}) copy-start(bf16[128,3,1024]{2,0,1:T(8,128)(2,1)} %param.7) | copy-start | bytes 2359300
  7.2 13.9 %copy-start.15 = (f32[3,3,1024]{2,1,0:T(4,128)S(1)}, f32[3,3,1024]{2,1,0:T(4,128)}, u32[]{:S(2)}) copy-start(f32[3,3,1024]{2,1,0:T(4,128)} %param.8) | copy-start | bytes 110596
  7.2 85.9 %all-gather.2.cloned.1.call-start = ((), (), s32[]{:S(2)}) async-start(), calls=%async_computation.5 | async-start | bytes 5242880 | tf_op jit(solution)/shard_map/all_gather | solution.py:130
  8.7 12.4 %collective-permute-start = (bf16[2,3,1024]{2,0,1:T(2,128)(2,1)S(1)}, bf16[2,3,1024]{2,0,1:T(2,128)(2,1)S(1)}, u32[]{:S(2)}, u32[]{:S(2)}) collective-permute-start(bf16[2,3,1024]{2,0,1:T(2,128)(2,1)S(1)} %slice.52), channel_id=1, source_target_pairs={{0,4},{4,8},{8,12},{1,5},{5,9},{9,13},{2,6},{6,10},{10,14},{3,7},{... | collective-permute-start | bytes 36872 | tf_op jit(solution)/shard_map/ppermute | solution.py:15
  21.7 80.3 %copy-start.13 = (f32[256,16]{0,1:T(8,128)S(1)}, f32[256,16]{0,1:T(8,128)}, u32[]{:S(2)}) copy-start(f32[256,16]{0,1:T(8,128)} %param.10) | copy-start | bytes 49156
  21.7 80.3 %copy-start.14 = (f32[256,16]{0,1:T(8,128)S(1)}, f32[256,16]{0,1:T(8,128)}, u32[]{:S(2)}) copy-start(f32[256,16]{0,1:T(8,128)} %param.9) | copy-start | bytes 49156
  98.3 12.6 %all-to-all-start.2 = ((bf16[4,256,128]{1,2,0:T(8,128)(2,1)}), bf16[4,256,128]{1,2,0:T(8,128)(2,1)S(1)}, u32[]{:S(2)}, u32[]{:S(2)}) async-start(bf16[4,256,128]{1,2,0:T(8,128)(2,1)} %bitcast.222), calls=%async_computation.2 | async-start | bytes 524288 | tf_op jit(solution)/shard_map/all_to_all | solution.py:137
  110.9 10.3 %all-to-all-start = ((bf16[4,256,128]{1,2,0:T(8,128)(2,1)}), bf16[4,256,128]{1,2,0:T(8,128)(2,1)S(1)}, u32[]{:S(2)}, u32[]{:S(2)}) async-start(bf16[4,256,128]{1,2,0:T(8,128)(2,1)} %bitcast.223), calls=%async_computation | async-start | bytes 524288 | tf_op jit(solution)/shard_map/all_to_all | solution.py:136
  114.4 253.4 %reduce-scatter.2.cloned.1.call-start = ((), (), s32[]{:S(2)}) async-start(), calls=%async_computation.6 | async-start | bytes 10485760 | tf_op jit(solution)/shard_map/reduce_scatter | solution.py:170
  121.2 1.9 copy-start.4
  121.3 1.8 copy-start.6
  121.3 1.8 copy-start.7
  136.0 1.8 copy-start
  137.9 3.1 copy-start.2
  173.5 1.9 copy-start.1
  173.5 1.9 copy-start.3
  173.5 1.9 copy-start.8
  202.7 1.0 copy-start.5
  202.7 0.9 copy-start.16
  219.9 3.6 copy-start.11
  219.9 16.8 %all-to-all-start.3 = ((bf16[256,4,128]{0,2,1:T(8,128)(2,1)}), bf16[256,4,128]{0,2,1:T(8,128)(2,1)S(1)}, u32[]{:S(2)}, u32[]{:S(2)}) async-start(bf16[256,4,128]{0,2,1:T(8,128)(2,1)} %bitcast.54), calls=%async_computation.3 | async-start | bytes 524288 | tf_op jit(solution)/shard_map/all_to_all | solution.py:145
  223.5 3.8 %copy-start.12 = (f32[256,16]{1,0:T(8,128)S(1)}, f32[256,16]{1,0:T(8,128)}, u32[]{:S(2)}) copy-start(f32[256,16]{1,0:T(8,128)} %get-tuple-element.15) | copy-start | bytes 49156
  238.2 8.9 %collective-permute-start.1 = (f32[2,3,1024]{2,0,1:T(2,128)S(1)}, f32[2,3,1024]{2,0,1:T(2,128)S(1)}, u32[]{:S(2)}, u32[]{:S(2)}) collective-permute-start(f32[2,3,1024]{2,0,1:T(2,128)S(1)} %slice.72), channel_id=1, source_target_pairs={{4,0},{8,4},{12,8},{5,1},{9,5},{13,9},{6,2},{10,6},{14,10},{7,3},{... | collective-permute-start | bytes 73736 | tf_op jit(solution)/shard_map/ppermute | solution.py:15
  240.1 7.2 %copy-start.10 = (bf16[128,3,1024]{2,0,1:T(8,128)(2,1)S(1)}, bf16[128,3,1024]{2,0,1:T(8,128)(2,1)}, u32[]{:S(2)}) copy-start(bf16[128,3,1024]{2,0,1:T(8,128)(2,1)} %param.7) | copy-start | bytes 2359300
Sparse Core Ops, SparseCore 0:
  9.6 83.4 all-gather.1
  220.1 147.5 reduce-scatter.1
where the time goes:
time: 381 us; the launch traced here: 378 us
  waiting for transfers between devices  194 us (51%)
  matrix products  81.8 us (21%)
  blocking collectives  37.7 us (10%)
  other arithmetic  21.3 us (6%)
  starting transfers between devices  16.8 us (4%)
  between operations  14.9 us (4%)
  local copies, waits for them, and re-layouts  11.7 us (3%)
    reduce_scatter x1, waiting for transfers between devices, body(): lax.psum_scatter(partial_term, 'ctx', scatter_dimension=1, tiled=True)  98.2 us
    all_gather x1, waiting for transfers between devices, body(): lax.all_gather(out_weight, 'ctx', axis=1, tiled=True)  71.3 us
    psum x1, blocking collectives, body(): grad_short = lax.psum(jnp.stack(short_terms, axis=0), 'ctx') / norm_factor  19.5 us
    dot_general x3, matrix products, inverse_dft(): jnp.einsum('ak,ckb->cab', a_sin, turn_imag, precision=highest)  11.5 us
    dot_general x3, matrix products, inverse_dft(): jnp.einsum('ak,ckb->cab', a_cos, turn_real, precision=highest)  11.1 us
    all_to_all x1, blocking collectives, body(): lax.all_to_all(mix_cols, 'ctx', split_axis=1, concat_axis=0, tiled=True)  10.8 us
    all_to_all x1, waiting for transfers between devices, body(): lax.all_to_all(grad_cols, 'ctx', split_axis=1, concat_axis=0, tiled=True)  8.56 us
  transfers between devices with their start and end apart: 7, of which 6 were waited for; matrix products, arithmetic and copies ran while one was open for 5% of the time, Pallas kernels for 0%

commit v1 on v0

--- a/solution.py
+++ b/solution.py
@@ -3,6 +3,7 @@
 
 import jax
 import jax.numpy as jnp
+import numpy as np
 from jax import lax
 from jax.sharding import PartitionSpec as P
 
@@ -110,7 +111,7 @@
     return (grad_cols, grad_filter, skip_sum)
 
 
-def body(projections, short_taps, residues, decay_rates, skip_gain, grad_mixed, out_weight):
+def body_factored(projections, short_taps, residues, decay_rates, skip_gain, grad_mixed, out_weight):
     tokens = projections.shape[0]
     seq_len = tokens * lax.axis_size("ctx")
     norm_factor = math.sqrt(seq_len)
@@ -169,6 +170,136 @@
     )
     weight_sum = lax.psum_scatter(partial_term, "ctx", scatter_dimension=1, tiled=True)
     grad_weight = weight_sum / norm_factor
+    return (grad_projections, grad_short, grad_skip, grad_residues, grad_log_rates, grad_weight)
+
+
+def wave_tables(seq_len):
+    fine = 16
+    steps = np.arange(seq_len, dtype=np.int64)[None, :]
+    coarse = np.arange(seq_len // fine, dtype=np.int64)[:, None] * (2 * fine)
+    inner = np.arange(fine, dtype=np.int64)[:, None] * 2 + 1
+    outs = []
+    for rows in (coarse, inner):
+        angle = (rows * steps % (4 * seq_len)) * (2.0 * math.pi / (4 * seq_len))
+        outs += [np.cos(angle).astype(np.float32), np.sin(angle).astype(np.float32)]
+    return outs
+
+
+def waves(tables):
+    ca, sa, cb, sb = tables
+    ca, sa = ca[:, None, :], sa[:, None, :]
+    cb, sb = cb[None], sb[None]
+    seq_len = ca.shape[-1]
+    cos = (ca * cb - sa * sb).reshape(seq_len, seq_len)
+    sin = (sa * cb + ca * sb).reshape(seq_len, seq_len)
+    return jnp.concatenate([cos, sin], axis=0)
+
+
+def dot0(a, b):
+    return lax.dot_general(a, b, (((0,), (0,)), ((), ())), preferred_element_type=jnp.float32)
+
+
+def dot1(a, b):
+    return lax.dot_general(a, b, (((1,), (0,)), ((), ())), preferred_element_type=jnp.float32)
+
+
+def split(x):
+    high = x.astype(jnp.bfloat16)
+    return high, (x - high.astype(jnp.float32)).astype(jnp.bfloat16)
+
+
+def shift_down(x, by):
+    return jnp.pad(x, ((by, 0), (0, 0)))[: x.shape[0]] if by else x
+
+
+def shift_up(x, by):
+    return jnp.pad(x, ((0, by), (0, 0)))[by:] if by else x
+
+
+def body(projections, short_taps, residues, decay_rates, skip_gain, grad_mixed, out_weight):
+    tokens, _, width = projections.shape
+    peers = lax.axis_size("ctx")
+    seq_len = tokens * peers
+    if seq_len > 1024:
+        return body_factored(
+            projections, short_taps, residues, decay_rates, skip_gain, grad_mixed, out_weight
+        )
+    cols = width // peers
+    me = lax.axis_index("ctx")
+    norm = math.sqrt(seq_len)
+    f32, bf16 = jnp.float32, jnp.bfloat16
+    proj = lax.all_to_all(
+        projections.transpose(1, 0, 2), "ctx", split_axis=2, concat_axis=1, tiled=True
+    )
+    weight = lax.all_to_all(out_weight, "ctx", split_axis=0, concat_axis=1, tiled=True)
+    gm = lax.all_gather(grad_mixed, "ch", axis=1, tiled=True)
+    gm = lax.all_gather(gm, "ctx", axis=0, tiled=True)
+    taps = lax.dynamic_slice_in_dim(short_taps, me * cols, cols, 2)
+    tables = lax.optimization_barrier([jnp.asarray(t) for t in wave_tables(seq_len)])
+    wave_h, wave_l = split(waves(tables))
+    rate = decay_rates.T
+    amp = jnp.sqrt(2.0 * rate / seq_len)
+    where = jnp.arange(seq_len, dtype=f32) / seq_len
+    filt = jnp.sum((residues.T * amp)[:, None, :] * jnp.exp(-rate[:, None, :] * where[None, :, None]), axis=0)
+
+    def forward_exact(x):
+        return dot1(wave_h, x) + dot1(wave_l, x)
+
+    def forward(x):
+        high, low = split(x)
+        return dot1(wave_h, high) + dot1(wave_l, high) + dot1(wave_h, low)
+
+    def backward(top, bottom):
+        high, low = split(jnp.concatenate([top, bottom], axis=0))
+        return (dot0(wave_h, high) + dot0(wave_l, high) + dot0(wave_h, low)) * (1.0 / seq_len)
+
+    def halves(x):
+        return x[:seq_len], x[seq_len:]
+
+    p, q = halves(forward(filt))
+    proj_f = [proj[g].astype(f32) for g in range(3)]
+    query, key, value = (
+        sum(taps[j, g][None] * shift_down(proj_f[g], j) for j in range(SHORT)) for g in range(3)
+    )
+    gated = (key * value).astype(bf16)
+    a, b = halves(forward_exact(gated))
+    gated_f = gated.astype(f32)
+    gain = skip_gain[None]
+    mix = (backward(p * a - q * b, p * b + q * a) + gain * gated_f).astype(bf16).astype(f32)
+    mixed_out = (query * mix).astype(bf16)
+    mixed_all = lax.all_gather(mixed_out, "ctx", axis=1, tiled=True)
+
+    grad_out = lax.dot_general(gm, weight, (((1,), (1,)), ((), ())), preferred_element_type=f32)
+    grad_y = (grad_out * query).astype(bf16)
+    grad_yf = grad_y.astype(f32)
+    d, e = halves(forward_exact(grad_y))
+    grad_gated = (backward(p * d + q * e, p * e - q * d) + gain * grad_yf).astype(bf16).astype(f32)
+    grad_filter = backward(d * a + e * b, e * a - d * b)
+    grad_skip = jnp.sum(grad_yf * gated_f, axis=0) / norm
+    basis = jnp.exp(-rate[:, None, :] * where[None, :, None]) * grad_filter[None]
+    moment0 = jnp.sum(basis, axis=1)
+    moment1 = jnp.sum(basis * where[None, :, None], axis=1)
+    grad_residues = (amp * moment0 / norm).T
+    grad_log_rates = (residues.T * amp * (0.5 * moment0 - rate * moment1) / norm).T
+    grad_mix = [grad_out * mix, grad_gated * value, grad_gated * key]
+    grad_proj = jnp.stack(
+        [
+            sum(taps[j, g][None] * shift_up(grad_mix[g], j) for j in range(SHORT)).astype(bf16)
+            for g in range(3)
+        ]
+    )
+    grad_projections = lax.all_to_all(
+        grad_proj, "ctx", split_axis=1, concat_axis=2, tiled=True
+    ).transpose(1, 0, 2)
+    short = jnp.stack(
+        [
+            jnp.stack([jnp.sum(grad_mix[g] * shift_down(proj_f[g], j), axis=0) for g in range(3)])
+            for j in range(SHORT)
+        ]
+    )
+    grad_short = lax.all_gather(short / norm, "ctx", axis=2, tiled=True)
+    gm_own = lax.dynamic_slice_in_dim(gm, me * (gm.shape[1] // peers), gm.shape[1] // peers, 1)
+    grad_weight = dot0(mixed_all, gm_own) / norm
     return (grad_projections, grad_short, grad_skip, grad_residues, grad_log_rates, grad_weight)
 
 

time: 381 us -> 194 us (0.51)
  waiting for transfers between devices: 194 us -> 20 us
  blocking collectives: 37.7 us -> 111 us
  matrix products: 81.8 us -> 17.8 us
  other arithmetic: 21.3 us -> 7.95 us
  starting transfers between devices: 16.8 us -> 7.85 us
    reduce_scatter x1 -> x0, waiting for transfers between devices: 98.2 us -> none  [body(): lax.psum_scatter(partial_term, 'ctx', scatter_dimension=1, tiled=True)]
    all_gather x1 -> x2, waiting for transfers between devices: 71.3 us -> 0.01 us  [the longest x1 0.01 us: body(): gm = lax.all_gather(gm, 'ctx', axis=0, tiled=True)]
    dot_general x38 -> x18, matrix products: 81.8 us -> 17.8 us  [the longest x10 10.4 us: dot0(): lax.dot_general(a, b, (((0,), (0,)), ((), ())), preferred_element_type=jn...]
    all_gather x1 -> x2, blocking collectives: 7.38 us -> 54 us  [the longest x1 43.8 us: body(): grad_short = lax.all_gather(short / norm, 'ctx', axis=2, tiled=True)]
    all_to_all x1, blocking collectives: 10.8 us -> 57.4 us  [body(): lax.all_to_all(projections.transpose(1, 0, 2), 'ctx', split_axis=2, conca...]
    psum x1 -> x0, blocking collectives: 19.5 us -> none  [body(): grad_short = lax.psum(jnp.stack(short_terms, axis=0), 'ctx') / norm_factor]
    ppermute x2 -> x0, waiting for transfers between devices: 7.04 us -> none  [from_behind(): return lax.ppermute(x, axis, pairs)]
    ppermute x2 -> x0, starting transfers between devices: 6.22 us -> none  [from_behind(): return lax.ppermute(x, axis, pairs)]
  transfers between devices with their start and end apart: 7 -> 4, of which waited for: 6 -> 1; matrix products, arithmetic and copies ran while one was open for 5% -> 8% of each run, Pallas kernels for 0% -> 0%
where the time goes in v1:
time: 194 us; the launch traced here: 193 us
  blocking collectives  111 us (57%)
  waiting for transfers between devices  20 us (10%)
  matrix products  17.8 us (9%)
  between operations  14.5 us (7%)
  local copies, waits for them, and re-layouts  13.7 us (7%)
  other arithmetic  7.95 us (4%)
  starting transfers between devices  7.85 us (4%)
    all_to_all x1, blocking collectives, body(): lax.all_to_all(projections.transpose(1, 0, 2), 'ctx', split_axis=2, conca...  57.4 us
    all_gather x1, blocking collectives, body(): grad_short = lax.all_gather(short / norm, 'ctx', axis=2, tiled=True)  43.8 us
    all_to_all x1, waiting for transfers between devices, body(): lax.all_to_all(out_weight, 'ctx', split_axis=0, concat_axis=1, tiled=True)  20 us
    dot_general x10, matrix products, dot0(): lax.dot_general(a, b, (((0,), (0,)), ((), ())), preferred_element_type=jn...  10.4 us
    all_gather x1, blocking collectives, body(): gm = lax.all_gather(grad_mixed, 'ch', axis=1, tiled=True)  10.2 us
    dot_general x1, matrix products, body(): lax.dot_general(gm, weight, (((1,), (1,)), ((), ())), preferred_element_t...  4.41 us
    all_to_all x1, starting transfers between devices, body(): lax.all_to_all(out_weight, 'ctx', split_axis=0, concat_axis=1, tiled=True)  4.25 us
    unnamed x42, local copies, waits for them, and re-layouts  4.2 us
  transfers between devices with their start and end apart: 4, of which 1 were waited for; matrix products, arithmetic and copies ran while one was open for 8% of the time, Pallas kernels for 0%

profile of v1, /device:TPU:0, one launch (start us, length us, event | category | flops | bytes accessed | tf_op | source)
XLA Modules:
  0.0 193.2 jit_solution(15678830938014121140)
XLA Ops:
  7.2 0.0 all-gather.3.cloned.1.call-start
  7.2 10.2 %all_gather.12 = bf16[128,2048]{1,0:T(8,128)(2,1)} all-gather(bf16[128,512]{1,0:T(8,128)(2,1)} %param.16), channel_id=1, replica_groups=mesh['groups'=2,'ctx'=4,'ch'=4] {'ch'}, dimensions={1}, use_global_device_ids=true | all-gather | bytes 655360 | tf_op jit(solution)/shard_map/all_gather | solution.py:235
  17.4 0.0 all-gather.3.cloned.1.call-update
  17.4 1.7 copy.30
  19.1 0.0 copy-start.11
  19.1 0.0 copy-start.12
  19.1 0.0 copy-start.15
  19.2 57.4 %all_to_all.52 = bf16[3,128,1024]{1,0,2:T(4,128)(2,1)S(1)} all-to-all(bf16[3,128,1024]{1,0,2:T(4,128)(2,1)S(1)} %bitcast.101), channel_id=1, replica_groups=mesh['groups'=2,'ctx'=4,'ch'=4] {'ctx'}, dimensions={2} | all-to-all | bytes 1572864 | tf_op jit(solution)/shard_map/all_to_all | solution.py:231
  76.5 4.3 %all-to-all-start = ((bf16[4,256,512]{2,1,0:T(8,128)(2,1)}), bf16[4,256,512]{2,1,0:T(8,128)(2,1)}, u32[]{:S(2)}, u32[]{:S(2)}) async-start(bf16[4,256,512]{2,1,0:T(8,128)(2,1)} %bitcast.1), calls=%async_computation | async-start | bytes 2097152 | tf_op jit(solution)/shard_map/all_to_all | solution.py:234
  80.8 0.0 all-gather.5.cloned.1.call-start
  80.8 0.9 constant_dynamic-slice_fusion.3
  81.8 0.3 multiply_subtract_fusion
  82.2 0.3 subtract_convert_fusion
  82.5 0.4 copy-done.13
  82.8 0.0 copy-done.14
  82.9 1.3 copy.31
  84.2 1.2 fusion.68
  85.4 0.9 bitcast_convert_fusion.2
  86.3 0.0 copy-done.4
  86.4 0.1 bitcast_convert_fusion
  86.5 20.0 %all-to-all-done = bf16[4,256,512]{2,1,0:T(8,128)(2,1)} async-done(((bf16[4,256,512]{2,1,0:T(8,128)(2,1)}), bf16[4,256,512]{2,1,0:T(8,128)(2,1)}, u32[]{:S(2)}, u32[]{:S(2)}) %all-to-all-start) | async-done | bytes 1048608 | tf_op jit(solution)/shard_map/all_to_all | solution.py:234
  106.5 2.3 %copy.29 = bf16[256,4,512]{0,2,1:T(8,128)(2,1)} copy(bf16[256,4,512]{2,0,1:T(8,128)(2,1)} %bitcast.2) | data formatting | bytes 2097152 | tf_op jit(solution)/shard_map/all_to_all | solution.py:234
  108.7 4.4 %fusion.30 = (f32[256]{0:T(256)S(1)}, bf16[512,256]{1,0:T(8,128)(2,1)S(1)}, f32[512,256]{1,0:T(8,128)}, f32[512,256]{1,0:T(8,128)}, bf16[512,256]{1,0:T(8,128)(2...) fusion(f32[512,256]{1,0:T(8,128)S(1)} %get-tuple-element.70, f32[256]{0:T(256)S(1)} %bitcast.107, ...), kind=kOutput, calls=%fused_computation.70 | convolution fusion | flops 539885312 | bytes 7350272 | tf_op jit(solution)/shard_map/dot_general | solution.py:272
  113.2 0.4 fusion.70
  113.6 0.4 fusion.69
  114.0 0.4 convolution_add_fusion
  114.5 0.4 convolution_add_fusion.1
  114.9 0.1 multiply_add_fusion.1
  115.1 0.5 fusion.45
  115.5 0.5 convolution_add_fusion.5
  116.0 0.5 fusion.5
  116.5 3.1 %multiply_reduce_fusion = (f32[16,256]{1,0:T(8,128)S(1)}, f32[16,256]{1,0:T(8,128)S(1)}, f32[512,256]{1,0:T(8,128)S(1)}) fusion(f32[512,256]{1,0:T(8,128)S(1)} %fusion.5, f32[512]{0:T(512)S(1)} %iota_multiply_fusion, f32[16,256]{1,0:T(8,128)S(1)} %get-tuple-element.67, f32[16,256]{1,0:T(8,128)S(1)} %get-tuple-element.66), kind=kLoop, calls=%fused_computation | loop fusion | flops 14540800 | bytes 1116160 | tf_op jit(solution)/shard_map/reduce_sum | solution.py:281
  119.6 0.4 fusion.65
  120.1 0.4 convolution_add_fusion.3
  120.5 0.4 convolution_add_fusion.2
  121.0 1.2 multiply_subtract_fusion.3
  122.2 0.5 fusion.37
  122.7 0.5 convolution_add_fusion.9
  123.2 0.2 copy-done.17
  123.3 1.4 multiply_reduce_fusion.7
  124.8 0.0 all-gather.5.cloned.1.call-update
  124.8 0.2 fusion.34
  125.0 1.8 fusion.41
  126.8 0.5 convolution_add_fusion.7
  127.3 0.4 copy-done.3
  127.7 0.1 copy-done.5
  127.8 0.1 copy-done.7
  127.9 0.2 copy-done.9
  128.1 0.2 copy-done.10
  128.2 0.2 copy-done.18
  128.4 0.2 copy-done.19
  128.5 0.9 multiply_reduce_fusion.6
  129.4 0.2 fusion.33
  129.6 0.2 fusion.32
  129.8 0.1 pad_maximum_fusion.4
  129.9 1.6 copy.32
  131.5 3.5 %all-to-all-start.2 = ((bf16[3,512,256]{2,0,1:T(4,128)(2,1)}), bf16[3,512,256]{2,0,1:T(4,128)(2,1)S(1)}, u32[]{:S(2)}, u32[]{:S(2)}) async-start(bf16[3,512,256]{2,0,1:T(4,128)(2,1)} %copy.32), calls=%async_computation.2 | async-start | bytes 2097152 | tf_op jit(solution)/shard_map/all_to_all | solution.py:291
  135.1 43.8 %all_gather.14 = f32[3,3,1024]{2,1,0:T(4,128)S(1)} all-gather(f32[3,3,256]{2,1,0:T(4,128)S(1)} %maximum_multiply_fusion), channel_id=1, replica_groups=mesh['groups'=2,'ctx'=4,'ch'=4] {'ctx'}, dimensions={2}, use_global_device_ids=true | all-gather | bytes 46080 | tf_op jit(solution)/shard_map/all_gather | solution.py:300
  178.9 0.6 broadcast_multiply_fusion
  179.5 0.6 fusion.49
  180.1 0.7 copy.33
  180.9 1.4 all_to_all.48
  182.3 3.4 %convolution_multiply_fusion = f32[1024,512]{1,0:T(8,128)} fusion(bf16[512,1024]{1,0:T(8,128)(2,1)} %all-gather.5.cloned.1.call-done, bf16[512,2048]{1,0:T(8,128)(2,1)} %all-gather.3.cloned.1.call-done, s32[]{:T(128)S(6)} %select_n.7), kind=kOutput, calls=%fused_computation.8 | convolution fusion | flops 537395200 | bytes 3670020 | tf_op jit(solution)/shard_map/dot_general | solution.py:199
  185.7 0.6 copy.35
  (35 shorter events, 0.1 us)
Async XLA Ops:
  7.2 101.6 %all-gather.3.cloned.1.call-start = ((), (), s32[]{:S(2)}) async-start(), calls=%async_computation.3 | async-start | bytes 2621440 | tf_op jit(solution)/shard_map/all_gather | solution.py:236
  19.1 62.7 %copy-start.11 = (f32[32,512]{1,0:T(8,128)S(1)}, f32[32,512]{1,0:T(8,128)}, u32[]{:S(2)}) copy-start(f32[32,512]{1,0:T(8,128)} %constant.50.clone) | copy-start | bytes 196612
  19.1 62.7 %copy-start.12 = (f32[32,512]{1,0:T(8,128)S(1)}, f32[32,512]{1,0:T(8,128)}, u32[]{:S(2)}) copy-start(f32[32,512]{1,0:T(8,128)} %constant.49.clone) | copy-start | bytes 196612
  19.1 62.7 %copy-start.15 = (f32[16,512]{1,0:T(8,128)S(1)}, f32[16,512]{1,0:T(8,128)}, u32[]{:S(2)}) copy-start(f32[16,512]{1,0:T(8,128)} %constant.52.clone) | copy-start | bytes 98308
  19.1 62.7 %copy-start.16 = (f32[16,512]{1,0:T(8,128)S(1)}, f32[16,512]{1,0:T(8,128)}, u32[]{:S(2)}) copy-start(f32[16,512]{1,0:T(8,128)} %constant.51.clone) | copy-start | bytes 98308
  76.5 30.0 %all-to-all-start = ((bf16[4,256,512]{2,1,0:T(8,128)(2,1)}), bf16[4,256,512]{2,1,0:T(8,128)(2,1)}, u32[]{:S(2)}, u32[]{:S(2)}) async-start(bf16[4,256,512]{2,1,0:T(8,128)(2,1)} %bitcast.1), calls=%async_computation | async-start | bytes 2097152 | tf_op jit(solution)/shard_map/all_to_all | solution.py:234
  80.8 101.5 %all-gather.5.cloned.1.call-start = ((), (), s32[]{:S(2)}) async-start(), calls=%async_computation.4 | async-start | bytes 1310720 | tf_op jit(solution)/shard_map/all_gather | solution.py:270
  82.1 0.7 copy-start.13
  82.1 0.7 copy-start.14
  85.4 0.9 copy-start.2
  85.4 1.0 copy-start.4
  86.5 26.7 %copy-start.8 = (f32[512,256]{1,0:T(8,128)}, f32[512,256]{1,0:T(8,128)S(1)}, u32[]{:S(2)}) copy-start(f32[512,256]{1,0:T(8,128)S(1)} %get-tuple-element.70) | copy-start | bytes 1572868
  113.2 0.9 copy-start.6
  122.7 0.7 copy-start.17
  124.8 2.0 %copy-start = (f32[512,256]{1,0:T(8,128)S(1)}, f32[512,256]{1,0:T(8,128)}, u32[]{:S(2)}) copy-start(f32[512,256]{1,0:T(8,128)} %get-tuple-element.43) | copy-start | bytes 1572868
  124.8 2.0 %copy-start.1 = (f32[512,256]{1,0:T(8,128)S(1)}, f32[512,256]{1,0:T(8,128)}, u32[]{:S(2)}) copy-start(f32[512,256]{1,0:T(8,128)} %get-tuple-element.44) | copy-start | bytes 1572868
  126.8 1.0 copy-start.3
  126.8 1.0 copy-start.5
  126.8 1.1 copy-start.7
  126.8 1.3 copy-start.9
  126.8 1.4 copy-start.10
  126.8 1.6 copy-start.18
  126.8 1.7 copy-start.19
  131.5 48.6 %all-to-all-start.2 = ((bf16[3,512,256]{2,0,1:T(4,128)(2,1)}), bf16[3,512,256]{2,0,1:T(4,128)(2,1)S(1)}, u32[]{:S(2)}, u32[]{:S(2)}) async-start(bf16[3,512,256]{2,0,1:T(4,128)(2,1)} %copy.32), calls=%async_computation.2 | async-start | bytes 2097152 | tf_op jit(solution)/shard_map/all_to_all | solution.py:291
Sparse Core Ops, SparseCore 0:
  17.6 77.7 all-gather.2
  124.9 45.2 all-gather.4

commit v2 on v0

--- a/solution.py
+++ b/solution.py
@@ -3,7 +3,10 @@
 
 import jax
 import jax.numpy as jnp
+import numpy as np
 from jax import lax
+from jax.experimental import pallas as pl
+from jax.experimental.pallas import tpu as pltpu
 from jax.sharding import PartitionSpec as P
 
 SHORT = 3
@@ -110,7 +113,7 @@
     return (grad_cols, grad_filter, skip_sum)
 
 
-def body(projections, short_taps, residues, decay_rates, skip_gain, grad_mixed, out_weight):
+def body_factored(projections, short_taps, residues, decay_rates, skip_gain, grad_mixed, out_weight):
     tokens = projections.shape[0]
     seq_len = tokens * lax.axis_size("ctx")
     norm_factor = math.sqrt(seq_len)
@@ -170,6 +173,362 @@
     weight_sum = lax.psum_scatter(partial_term, "ctx", scatter_dimension=1, tiled=True)
     grad_weight = weight_sum / norm_factor
     return (grad_projections, grad_short, grad_skip, grad_residues, grad_log_rates, grad_weight)
+
+
+MESH = pl.DeviceIdType.MESH
+FINE = 16
+ROWS = 64
+PAD = 8
+
+
+def wave_tables(seq_len):
+    odd = np.arange(seq_len, dtype=np.int64)[None, :] * 2 + 1
+    steps = np.arange(seq_len, dtype=np.int64)[None, :]
+    coarse = np.arange(seq_len // FINE, dtype=np.int64)[:, None] * FINE
+    fine = np.arange(FINE, dtype=np.int64)[:, None]
+    rows = []
+    for product in (2 * coarse * steps, (2 * fine + 1) * steps, coarse * odd, fine * odd):
+        angle = (product % (4 * seq_len)) * (2.0 * math.pi / (4 * seq_len))
+        rows += [np.cos(angle), np.sin(angle)]
+    return np.concatenate(rows, axis=0).astype(np.float32)
+
+
+def dot(a, b):
+    return lax.dot_general(a, b, (((1,), (0,)), ((), ())), preferred_element_type=jnp.float32)
+
+
+def mega(
+    proj, w, gm, taps, gain, res, rate, tab,
+    o_proj, o_short, o_skip, o_res, o_rate, o_weight,
+    pbuf, wbuf, gbuf, mbuf, gp, short_own,
+    wh, wl, th, tl, pq, ab, de, sp_h, sp_l, x_h, x_l,
+    pf, qkv, gated, gmix, gout, mix, filt, gy, gf,
+    loc, s_p, r_p, s_g, r_g, s_gf, r_gf, s_w, r_w, s_wf, r_wf, s_m, r_m, s_o, r_o, s_s, r_s,
+):
+    f32, bf16 = jnp.float32, jnp.bfloat16
+    peers = lax.axis_size("ctx")
+    tokens, cols = proj.shape[1], proj.shape[2] // peers
+    seq = tokens * peers
+    wide = gm.shape[1]
+    half = cols // 2
+    z = lax.axis_index("ctx")
+    k = lax.axis_index("ch")
+    g = lax.axis_index("groups")
+    norm = math.sqrt(seq)
+    hops = range(1, peers)
+
+    def ring(i, d):
+        return lax.rem(i + d + peers, peers)
+
+    def span(i, n):
+        return pl.ds(pl.multiple_of(i * n, n), n)
+
+    barrier = pltpu.get_barrier_semaphore()
+    for d in hops:
+        pl.semaphore_signal(barrier, inc=1, device_id={"ctx": ring(z, d)}, device_id_type=MESH)
+        pl.semaphore_signal(barrier, inc=1, device_id={"ch": ring(k, d)}, device_id_type=MESH)
+    pl.semaphore_signal(barrier, inc=1, device_id={"groups": 1 - g}, device_id_type=MESH)
+
+    def remote(src, dst, ssem, rsem, **where):
+        return pltpu.make_async_remote_copy(
+            src_ref=src, dst_ref=dst, send_sem=ssem, recv_sem=rsem,
+            device_id=where, device_id_type=MESH,
+        )
+
+    local = [
+        pltpu.make_async_copy(proj.at[:, :, span(z, cols)], pbuf.at[:, span(z, tokens), :], loc.at[0]),
+        pltpu.make_async_copy(gm, gbuf.at[k, span(z, tokens), :], loc.at[1]),
+        pltpu.make_async_copy(w.at[span(z, cols), :], wbuf.at[z], loc.at[2]),
+    ]
+    for c in local:
+        c.start()
+    pl.semaphore_wait(barrier, 2 * (peers - 1) + 1)
+
+    order = (2, 1, 3) if peers == 4 else tuple(hops)
+    c_p, c_g, c_w, c_gf, c_wf = {}, {}, {}, {}, {}
+    for d in order:
+        zp = ring(z, d)
+        c_p[d] = remote(proj.at[:, :, span(zp, cols)], pbuf.at[:, span(z, tokens), :], s_p.at[d - 1], r_p.at[d - 1], ctx=zp)
+        c_p[d].start()
+    for d in order:
+        zp = ring(z, d)
+        c_g[d] = remote(gm, gbuf.at[k, span(z, tokens), :], s_g.at[d - 1], r_g.at[d - 1], ctx=zp)
+        c_g[d].start()
+    for d in order:
+        zp = ring(z, d)
+        c_w[d] = remote(
+            w.at[pl.ds(pl.multiple_of(zp * cols + g * half, half), half), :],
+            wbuf.at[z, span(g, half), :], s_w.at[d - 1], r_w.at[d - 1], ctx=zp,
+        )
+        c_w[d].start()
+    for e in hops:
+        c_gf[0, e] = remote(gm, gbuf.at[k, span(z, tokens), :], s_gf.at[e - 1], r_gf.at[e - 1], ch=ring(k, e))
+        c_gf[0, e].start()
+
+    groups_of = seq // FINE
+    at = [0]
+    for n in (groups_of, groups_of, FINE, FINE, groups_of, groups_of, FINE, FINE):
+        at.append(at[-1] + n)
+
+    def put(high, low, rows, columns, x):
+        top = x.astype(bf16)
+        high[rows, columns] = top
+        low[rows, columns] = (x - top.astype(f32)).astype(bf16)
+
+    def fill(i, carry):
+        for base, high, low, by_row in ((0, wh, wl, True), (4, th, tl, False)):
+            ca, sa = tab[pl.ds(at[base] + i, 1), :], tab[pl.ds(at[base + 1] + i, 1), :]
+            cb, sb = tab[at[base + 2] : at[base + 3], :], tab[at[base + 3] : at[base + 4], :]
+            cos, sin = ca * cb - sa * sb, sa * cb + ca * sb
+            first = pl.multiple_of(i * FINE, FINE)
+            if by_row:
+                put(high, low, pl.ds(first, FINE), slice(None), cos)
+                put(high, low, pl.ds(pl.multiple_of(seq + i * FINE, FINE), FINE), slice(None), sin)
+            else:
+                put(high, low, pl.ds(first, FINE), slice(0, seq), cos)
+                put(high, low, pl.ds(first, FINE), slice(seq, 2 * seq), sin)
+        return carry
+
+    lax.fori_loop(0, groups_of, fill, 0)
+
+    order_n = res.shape[0]
+    amp = jnp.sqrt(2.0 * rate[...] / seq)
+    scaled = res[...] * amp
+    for r in range(0, seq, ROWS):
+        where = (lax.broadcasted_iota(jnp.int32, (ROWS, cols), 0) + r).astype(f32) / seq
+        total = jnp.zeros((ROWS, cols), f32)
+        for n in range(order_n):
+            total = total + scaled[n : n + 1] * jnp.exp(-rate[n : n + 1, :] * where)
+        put(x_h, x_l, slice(r, r + ROWS), slice(None), total)
+    block = 256
+    for r in range(0, 2 * seq, block):
+        rows = slice(r, r + block)
+        pq[rows] = dot(wh[rows], x_h[...]) + dot(wl[rows], x_h[...]) + dot(wh[rows], x_l[...])
+
+    def spectrum(out, x):
+        for r in range(0, 2 * seq, block):
+            rows = slice(r, r + block)
+            out[rows] = dot(wh[rows], x[...]) + dot(wl[rows], x[...])
+
+    def product(x, y, conj):
+        for r in range(0, seq, ROWS):
+            lo, hi = slice(r, r + ROWS), slice(seq + r, seq + r + ROWS)
+            a, b, c, d = x[lo], x[hi], y[lo], y[hi]
+            if conj:
+                put(sp_h, sp_l, lo, slice(None), a * c + b * d)
+                put(sp_h, sp_l, hi, slice(None), a * d - b * c)
+            else:
+                put(sp_h, sp_l, lo, slice(None), a * c - b * d)
+                put(sp_h, sp_l, hi, slice(None), a * d + b * c)
+
+    def inverse(r, n):
+        rows = slice(r, r + n)
+        total = dot(th[rows], sp_h[...]) + dot(tl[rows], sp_h[...]) + dot(th[rows], sp_l[...])
+        return total * (1.0 / seq)
+
+    for i in range(3):
+        pf[i, 0:PAD] = jnp.zeros((PAD, cols), f32)
+        gmix[i, seq : seq + PAD] = jnp.zeros((PAD, cols), f32)
+    gain_row = gain[...]
+
+    local[0].wait()
+    for d in order:
+        c_p[d].wait_recv()
+    for r in range(0, seq, ROWS):
+        for i in range(3):
+            pf[i, PAD + r : PAD + r + ROWS] = pbuf[i, r : r + ROWS].astype(f32)
+        for i in range(3):
+            total = jnp.zeros((ROWS, cols), f32)
+            for j in range(SHORT):
+                total = total + taps[3 * j + i : 3 * j + i + 1] * pf[i, PAD + r - j : PAD + r - j + ROWS]
+            qkv[i, r : r + ROWS] = total
+        gated[r : r + ROWS] = (qkv[1, r : r + ROWS] * qkv[2, r : r + ROWS]).astype(bf16)
+    spectrum(ab, gated)
+    product(pq, ab, False)
+    for r in range(0, seq, block):
+        rows = slice(r, r + block)
+        m = (inverse(r, block) + gain_row * gated[rows].astype(f32)).astype(bf16).astype(f32)
+        mix[rows] = m
+        mbuf[z, :, rows] = (qkv[0, rows] * m).T.astype(bf16)
+
+    local[1].wait()
+    local[2].wait()
+    for d in order:
+        c_g[d].wait_recv()
+        zs = ring(z, -d)
+        for e in hops:
+            part = gbuf.at[k, span(zs, tokens), :]
+            i = d * (peers - 1) + e - 1
+            c_gf[d, e] = remote(part, part, s_gf.at[i], r_gf.at[i], ch=ring(k, e))
+            c_gf[d, e].start()
+    for d in order:
+        c_w[d].wait_recv()
+        part = wbuf.at[ring(z, -d), span(g, half), :]
+        c_wf[d] = remote(part, part, s_wf.at[d - 1], r_wf.at[d - 1], groups=1 - g)
+        c_wf[d].start()
+    c_m = {}
+    for d in order:
+        c_m[d] = remote(mbuf.at[z], mbuf.at[z], s_m.at[d - 1], r_m.at[d - 1], ctx=ring(z, d))
+        c_m[d].start()
+    for key in c_gf:
+        c_gf[key].wait_recv()
+    for d in order:
+        c_wf[d].wait_recv()
+
+    for r in range(0, seq, block):
+        rows = slice(r, r + block)
+        total = jnp.zeros((block, cols), f32)
+        for j in range(peers):
+            total = total + lax.dot_general(
+                gbuf[j, rows, :], wbuf[j], (((1,), (1,)), ((), ())), preferred_element_type=f32
+            )
+        gout[rows] = total
+    for r in range(0, seq, ROWS):
+        rows = slice(r, r + ROWS)
+        go = gout[rows]
+        gy[rows] = (go * qkv[0, rows]).astype(bf16)
+        gmix[0, rows] = go * mix[rows]
+    spectrum(de, gy)
+    product(pq, de, True)
+    for r in range(0, seq, block):
+        rows = slice(r, r + block)
+        gg = (inverse(r, block) + gain_row * gy[rows].astype(f32)).astype(bf16).astype(f32)
+        gmix[1, rows] = gg * qkv[2, rows]
+        gmix[2, rows] = gg * qkv[1, rows]
+    for r in range(0, seq, ROWS):
+        for i in range(3):
+            total = jnp.zeros((ROWS, cols), f32)
+            for j in range(SHORT):
+                total = total + taps[3 * j + i : 3 * j + i + 1] * gmix[i, r + j : r + j + ROWS]
+            gp[i, r : r + ROWS] = total.astype(bf16)
+    c_o, c_s = {}, {}
+    for d in order:
+        zp = ring(z, d)
+        c_o[d] = remote(gp.at[:, span(zp, tokens), :], o_proj.at[:, :, span(z, cols)], s_o.at[d - 1], r_o.at[d - 1], ctx=zp)
+        c_o[d].start()
+    own = pltpu.make_async_copy(gp.at[:, span(z, tokens), :], o_proj.at[:, :, span(z, cols)], loc.at[3])
+    own.start()
+
+    def fold(x):
+        return jnp.sum(x.reshape(ROWS // 8, 8, cols), axis=0)
+
+    for i in range(3):
+        sums = [jnp.zeros((8, cols), f32) for _ in range(SHORT)]
+        for r in range(0, seq, ROWS):
+            here = gmix[i, r : r + ROWS]
+            for j in range(SHORT):
+                sums[j] = sums[j] + fold(here * pf[i, PAD + r - j : PAD + r - j + ROWS])
+        for j in range(SHORT):
+            short_own[3 * j + i : 3 * j + i + 1, :] = jnp.sum(sums[j], axis=0, keepdims=True) / norm
+    for j in range(9, 16):
+        short_own[j : j + 1, :] = jnp.zeros((1, cols), f32)
+    for d in order:
+        c_s[d] = remote(short_own, o_short.at[:, span(z, cols)], s_s.at[d - 1], r_s.at[d - 1], ctx=ring(z, d))
+        c_s[d].start()
+    own_short = pltpu.make_async_copy(short_own, o_short.at[:, span(z, cols)], loc.at[4])
+    own_short.start()
+    skip = jnp.zeros((8, cols), f32)
+    for r in range(0, seq, ROWS):
+        rows = slice(r, r + ROWS)
+        skip = skip + fold(gy[rows].astype(f32) * gated[rows].astype(f32))
+    o_skip[...] = jnp.sum(skip, axis=0, keepdims=True) / norm
+    product(ab, de, True)
+    for r in range(0, seq, block):
+        gf[r : r + block] = inverse(r, block)
+
+    def moments(n, carry):
+        decay = rate[pl.ds(n, 1), :]
+        sum0 = jnp.zeros((8, cols), f32)
+        sum1 = jnp.zeros((8, cols), f32)
+        for r in range(0, seq, ROWS):
+            where = (lax.broadcasted_iota(jnp.int32, (ROWS, cols), 0) + r).astype(f32) / seq
+            term = jnp.exp(-decay * where) * gf[r : r + ROWS]
+            sum0 = sum0 + fold(term)
+            sum1 = sum1 + fold(term * where)
+        m0 = jnp.sum(sum0, axis=0, keepdims=True)
+        m1 = jnp.sum(sum1, axis=0, keepdims=True)
+        size = jnp.sqrt(2.0 * decay / seq)
+        o_res[pl.ds(n, 1), :] = size * m0 / norm
+        o_rate[pl.ds(n, 1), :] = res[pl.ds(n, 1), :] * size * (0.5 * m0 - decay * m1) / norm
+        return carry
+
+    lax.fori_loop(0, order_n, moments, 0)
+
+    def weight(zs):
+        o_weight[span(zs, cols), :] = dot(mbuf[zs], gbuf[z]) * (1.0 / norm)
+
+    weight(z)
+    for d in (1, 3, 2) if peers == 4 else hops:
+        c_m[d].wait_recv()
+        weight(ring(z, -d))
+    for group in (c_o, c_s):
+        for d in order:
+            group[d].wait_recv()
+    own.wait()
+    own_short.wait()
+    for group in (c_p, c_g, c_w, c_gf, c_wf, c_m, c_o, c_s):
+        for key in group:
+            group[key].wait_send()
+
+
+def body(projections, short_taps, residues, decay_rates, skip_gain, grad_mixed, out_weight):
+    tokens, _, width = projections.shape
+    peers = lax.axis_size("ctx")
+    seq = tokens * peers
+    if seq > 1024 or lax.axis_size("ch") != peers or lax.axis_size("groups") != 2:
+        return body_factored(
+            projections, short_taps, residues, decay_rates, skip_gain, grad_mixed, out_weight
+        )
+    cols = width // peers
+    wide = grad_mixed.shape[1]
+    f32, bf16 = jnp.float32, jnp.bfloat16
+    taps = lax.dynamic_slice_in_dim(short_taps, lax.axis_index("ctx") * cols, cols, 2)
+    taps = taps.reshape(SHORT * 3, cols)
+    tables = jnp.asarray(wave_tables(seq))
+    order = residues.shape[1]
+    vmem = pl.BlockSpec(memory_space=pltpu.VMEM)
+    any_ = pl.BlockSpec(memory_space=pl.ANY)
+    near = peers - 1
+    dma = pltpu.SemaphoreType.DMA
+    S = jax.ShapeDtypeStruct
+    V = pltpu.VMEM
+    outs = pl.pallas_call(
+        mega,
+        out_shape=(
+            S((3, tokens, width), bf16), S((16, width), f32), S((1, cols), f32),
+            S((order, cols), f32), S((order, cols), f32), S((width, wide), f32),
+        ),
+        in_specs=[any_, any_, any_] + [vmem] * 5,
+        out_specs=[vmem] * 6,
+        scratch_shapes=[
+            V((3, seq, cols), bf16), V((peers, cols, wide), bf16), V((peers, seq, wide), bf16),
+            V((peers, cols, seq), bf16), V((3, seq, cols), bf16), V((16, cols), f32),
+            V((2 * seq, seq), bf16), V((2 * seq, seq), bf16), V((seq, 2 * seq), bf16), V((seq, 2 * seq), bf16),
+            V((2 * seq, cols), f32), V((2 * seq, cols), f32), V((2 * seq, cols), f32),
+            V((2 * seq, cols), bf16), V((2 * seq, cols), bf16), V((seq, cols), bf16), V((seq, cols), bf16),
+            V((3, PAD + seq, cols), f32), V((3, seq, cols), f32), V((seq, cols), bf16),
+            V((3, seq + PAD, cols), f32), V((seq, cols), f32), V((seq, cols), f32), V((8, cols), f32),
+            V((seq, cols), bf16), V((seq, cols), f32),
+            dma((5,)), dma((near,)), dma((near,)), dma((near,)), dma((near,)),
+            dma((peers * near,)), dma((peers * near,)), dma((near,)), dma((near,)), dma((near,)), dma((near,)),
+            dma((near,)), dma((near,)), dma((near,)), dma((near,)), dma((near,)), dma((near,)),
+        ],
+        compiler_params=pltpu.CompilerParams(
+            collective_id=0, has_side_effects=True, vmem_limit_bytes=56 * 1024 * 1024
+        ),
+    )(
+        projections.transpose(1, 0, 2), out_weight, grad_mixed, taps, skip_gain[None],
+        residues.T, decay_rates.T, tables,
+    )
+    grad_proj, short, skip, grad_res, grad_rate, grad_weight = outs
+    return (
+        grad_proj.transpose(1, 0, 2),
+        short[: SHORT * 3].reshape(SHORT, 3, width),
+        skip[0],
+        grad_res.T,
+        grad_rate.T,
+        grad_weight,
+    )
 
 
 def solution(mesh):

time: 381 us -> 104 us (0.27)
  waiting for transfers between devices: 194 us -> 0 us
  Pallas kernels: 0 us -> 90.1 us
  matrix products: 81.8 us -> 0 us
  blocking collectives: 37.7 us -> 0 us
  other arithmetic: 21.3 us -> 0 us
  starting transfers between devices: 16.8 us -> 0 us
  between operations: 14.9 us -> 0.66 us
    reduce_scatter x1 -> x0, waiting for transfers between devices: 98.2 us -> none  [body(): lax.psum_scatter(partial_term, 'ctx', scatter_dimension=1, tiled=True)]
    pallas_call x0 -> x1, Pallas kernels: none -> 90.1 us  [body(): pl.pallas_call(mega, out_shape=(S((3, tokens, width), bf16), S((16, width...]
    dot_general x38 -> x0, matrix products: 81.8 us -> none  [the longest x3 11.5 us: inverse_dft(): jnp.einsum('ak,ckb->cab', a_sin, turn_imag, precision=highest)]
    all_gather x1 -> x0, waiting for transfers between devices: 71.3 us -> none  [body(): lax.all_gather(out_weight, 'ctx', axis=1, tiled=True)]
    psum x1 -> x0, blocking collectives: 19.5 us -> none  [body(): grad_short = lax.psum(jnp.stack(short_terms, axis=0), 'ctx') / norm_factor]
    all_to_all x3 -> x0, waiting for transfers between devices: 16.4 us -> none  [the longest x1 8.56 us: body(): lax.all_to_all(grad_cols, 'ctx', split_axis=1, concat_axis=0, tiled=True)]
    all_to_all x1 -> x0, blocking collectives: 10.8 us -> none  [body(): lax.all_to_all(mix_cols, 'ctx', split_axis=1, concat_axis=0, tiled=True)]
    all_to_all x3 -> x0, starting transfers between devices: 10.4 us -> none  [the longest x1 3.55 us: body(): lax.all_to_all(grad_cols, 'ctx', split_axis=1, concat_axis=0, tiled=True)]
  transfers between devices with their start and end apart: 7 -> 0, of which waited for: 6 -> 0; matrix products, arithmetic and copies ran while one was open for 5% -> 0% of each run, Pallas kernels for 0% -> 0%
where the time goes in v2:
time: 104 us; the launch traced here: 103 us
  Pallas kernels  90.1 us (87%)
  local copies, waits for them, and re-layouts  11.9 us (11%)
    pallas_call x1, Pallas kernels, body(): pl.pallas_call(mega, out_shape=(S((3, tokens, width), bf16), S((16, width...  90.1 us
    unnamed x7, local copies, waits for them, and re-layouts  9.8 us

profile of v2, /device:TPU:0, one launch (start us, length us, event | category | flops | bytes accessed | tf_op | source)
XLA Modules:
  0.0 102.6 jit_solution(17233991752346944993)
XLA Ops:
  0.6 0.0 copy-start
  0.7 0.8 copy-done
  1.4 0.6 reshape.18.taps
  2.1 90.1 %shard_map.127 = (bf16[3,128,1024]{2,1,0:T(8,128)(2,1)}, f32[16,1024]{1,0:T(8,128)}, f32[1,256]{1,0:T(1,128)}, f32[16,256]{1,0:T(8,128)}, f32[16,256]{1,0:T(8,128)}, /*index=5*/f32[1024,512]{1,0:T(8,128)}) custom-call(bf16[3,128,1024]{2,1,0:T(8,128)(2,1)} %bitcast.10, bf16[1024,512]{1,0:T(8,128)(2,1)} %w.1, bf16[128,512]{1,0:T(8,128)(2,1)} %gm.1, ...), custom_call_target="tpu_custom_call" | custom-call | tf_op jit(solution)/shard_map/pallas_call | solution.py:495
  92.2 1.5 %reshape.19 = f32[3,3,1024]{2,1,0:T(4,128)} reshape(f32[9,1024]{1,0:T(8,128)} %bitcast.11) | data formatting | bytes 73728 | tf_op jit(solution)/shard_map/reshape | solution.py:526
  93.6 2.1 %copy.19 = bf16[128,3,1024]{2,0,1:T(8,128)(2,1)} copy(bf16[128,3,1024]{2,0,1:T(8,128)(2,1)} %bitcast.9) | data formatting | bytes 1572864
  95.7 1.2 %copy.20 = f32[256]{0:T(256)} copy(f32[256]{0:T(256)} %bitcast.17) | data formatting | bytes 2048
  96.9 1.3 %copy.21 = f32[256,16]{0,1:T(8,128)} copy(f32[256,16]{0,1:T(8,128)} %bitcast.15) | data formatting | bytes 32768
  98.2 1.3 %copy.22 = f32[256,16]{0,1:T(8,128)} copy(f32[256,16]{0,1:T(8,128)} %bitcast.14) | data formatting | bytes 32768
  99.6 3.1 %copy.23 = f32[1024,512]{1,0:T(8,128)} copy(f32[1024,512]{1,0:T(8,128)} %get-tuple-element.29) | data formatting | bytes 4194304
  (1 shorter events, 0.0 us)
Async XLA Ops:
  0.6 0.8 copy-start

commit v3 on v2

--- a/solution.py
+++ b/solution.py
@@ -244,16 +244,68 @@
         c.start()
     pl.semaphore_wait(barrier, 2 * (peers - 1) + 1)
 
-    order = (2, 1, 3) if peers == 4 else tuple(hops)
-    c_p, c_g, c_w, c_gf, c_wf = {}, {}, {}, {}, {}
+    order = (2, 1, 3)
+    c_p, c_w, c_wf = {}, {}, {}
+    mate = k + 1 - 2 * lax.rem(k, 2)
+    across = lax.rem(k + 2, 4)
+
+    def line(i, side, block, ssem, rsem):
+        slot = block(ring(z, -side * i))
+        sem = i if side > 0 else peers - 1 + i
+        return remote(slot, slot, ssem.at[sem], rsem.at[sem], ctx=ring(z, side))
+
+    def line_sends(i, side):
+        return (z + 1 < peers) & (z >= i) if side > 0 else (z >= 1) & (z + i < peers)
+
+    def line_gets(i, side):
+        return z >= i + 1 if side > 0 else z + i + 1 < peers
+
+    def line_start(i, block, ssem, rsem):
+        for side in (1, -1):
+            @pl.when(line_sends(i, side))
+            def _():
+                line(i, side, block, ssem, rsem).start()
+
+    def line_step(i, block, ssem, rsem, then=None):
+        for side in (1, -1):
+            @pl.when(line_gets(i, side))
+            def _():
+                line(i, side, block, ssem, rsem).wait_recv()
+                if then is not None:
+                    then(ring(z, -side * (i + 1)))
+        if i + 1 < peers - 1:
+            line_start(i + 1, block, ssem, rsem)
+
+    def line_end(block, ssem, rsem):
+        for i in range(peers - 1):
+            for side in (1, -1):
+                @pl.when(line_sends(i, side))
+                def _():
+                    line(i, side, block, ssem, rsem).wait_send()
+
+    def gm_block(zs):
+        return gbuf.at[k, span(zs, tokens), :]
+
+    def gm_out(zs, where):
+        n = zs + peers * where
+        column = (k, k, across)[where]
+        part = gbuf.at[column, span(zs, tokens), :]
+        return remote(part, part, s_gf.at[n], r_gf.at[n], ch=(mate, across, mate)[where])
+
+    def gm_spread(zs):
+        gm_out(zs, 1).start()
+        gm_out(zs, 0).start()
+
+    def mixed_block(zs):
+        return mbuf.at[zs]
+
+    local[1].wait()
+    line_start(0, gm_block, s_g, r_g)
+    gm_spread(z)
     for d in order:
         zp = ring(z, d)
         c_p[d] = remote(proj.at[:, :, span(zp, cols)], pbuf.at[:, span(z, tokens), :], s_p.at[d - 1], r_p.at[d - 1], ctx=zp)
         c_p[d].start()
-    for d in order:
-        zp = ring(z, d)
-        c_g[d] = remote(gm, gbuf.at[k, span(z, tokens), :], s_g.at[d - 1], r_g.at[d - 1], ctx=zp)
-        c_g[d].start()
     for d in order:
         zp = ring(z, d)
         c_w[d] = remote(
@@ -261,10 +313,6 @@
             wbuf.at[z, span(g, half), :], s_w.at[d - 1], r_w.at[d - 1], ctx=zp,
         )
         c_w[d].start()
-    for e in hops:
-        c_gf[0, e] = remote(gm, gbuf.at[k, span(z, tokens), :], s_gf.at[e - 1], r_gf.at[e - 1], ch=ring(k, e))
-        c_gf[0, e].start()
-
     groups_of = seq // FINE
     at = [0]
     for n in (groups_of, groups_of, FINE, FINE, groups_of, groups_of, FINE, FINE):
@@ -290,6 +338,7 @@
         return carry
 
     lax.fori_loop(0, groups_of, fill, 0)
+    line_step(0, gm_block, s_g, r_g, gm_spread)
 
     order_n = res.shape[0]
     amp = jnp.sqrt(2.0 * rate[...] / seq)
@@ -300,10 +349,13 @@
         for n in range(order_n):
             total = total + scaled[n : n + 1] * jnp.exp(-rate[n : n + 1, :] * where)
         put(x_h, x_l, slice(r, r + ROWS), slice(None), total)
+    line_step(1, gm_block, s_g, r_g, gm_spread)
     block = 256
     for r in range(0, 2 * seq, block):
         rows = slice(r, r + block)
         pq[rows] = dot(wh[rows], x_h[...]) + dot(wl[rows], x_h[...]) + dot(wh[rows], x_l[...])
+
+    line_step(2, gm_block, s_g, r_g, gm_spread)
 
     def spectrum(out, x):
         for r in range(0, 2 * seq, block):
@@ -351,27 +403,20 @@
         mix[rows] = m
         mbuf[z, :, rows] = (qkv[0, rows] * m).T.astype(bf16)
 
-    local[1].wait()
+    line_start(0, mixed_block, s_m, r_m)
     local[2].wait()
-    for d in order:
-        c_g[d].wait_recv()
-        zs = ring(z, -d)
-        for e in hops:
-            part = gbuf.at[k, span(zs, tokens), :]
-            i = d * (peers - 1) + e - 1
-            c_gf[d, e] = remote(part, part, s_gf.at[i], r_gf.at[i], ch=ring(k, e))
-            c_gf[d, e].start()
+    for zs in range(peers):
+        gm_out(zs, 1).wait_recv()
+        gm_out(zs, 2).start()
     for d in order:
         c_w[d].wait_recv()
         part = wbuf.at[ring(z, -d), span(g, half), :]
         c_wf[d] = remote(part, part, s_wf.at[d - 1], r_wf.at[d - 1], groups=1 - g)
         c_wf[d].start()
-    c_m = {}
-    for d in order:
-        c_m[d] = remote(mbuf.at[z], mbuf.at[z], s_m.at[d - 1], r_m.at[d - 1], ctx=ring(z, d))
-        c_m[d].start()
-    for key in c_gf:
-        c_gf[key].wait_recv()
+    line_step(0, mixed_block, s_m, r_m)
+    for zs in range(peers):
+        gm_out(zs, 0).wait_recv()
+        gm_out(zs, 2).wait_recv()
     for d in order:
         c_wf[d].wait_recv()
 
@@ -390,6 +435,7 @@
         gmix[0, rows] = go * mix[rows]
     spectrum(de, gy)
     product(pq, de, True)
+    line_step(1, mixed_block, s_m, r_m)
     for r in range(0, seq, block):
         rows = slice(r, r + block)
         gg = (inverse(r, block) + gain_row * gy[rows].astype(f32)).astype(bf16).astype(f32)
@@ -458,15 +504,20 @@
         o_weight[span(zs, cols), :] = dot(mbuf[zs], gbuf[z]) * (1.0 / norm)
 
     weight(z)
-    for d in (1, 3, 2) if peers == 4 else hops:
-        c_m[d].wait_recv()
-        weight(ring(z, -d))
+    line_step(2, mixed_block, s_m, r_m)
+    for d in hops:
+        weight(ring(z, d))
     for group in (c_o, c_s):
         for d in order:
             group[d].wait_recv()
     own.wait()
     own_short.wait()
-    for group in (c_p, c_g, c_w, c_gf, c_wf, c_m, c_o, c_s):
+    line_end(gm_block, s_g, r_g)
+    line_end(mixed_block, s_m, r_m)
+    for zs in range(peers):
+        for where in range(3):
+            gm_out(zs, where).wait_send()
+    for group in (c_p, c_w, c_wf, c_o, c_s):
         for key in group:
             group[key].wait_send()
 
@@ -475,7 +526,7 @@
     tokens, _, width = projections.shape
     peers = lax.axis_size("ctx")
     seq = tokens * peers
-    if seq > 1024 or lax.axis_size("ch") != peers or lax.axis_size("groups") != 2:
+    if seq > 1024 or peers != 4 or lax.axis_size("ch") != 4 or lax.axis_size("groups") != 2:
         return body_factored(
             projections, short_taps, residues, decay_rates, skip_gain, grad_mixed, out_weight
         )
@@ -509,9 +560,9 @@
             V((3, PAD + seq, cols), f32), V((3, seq, cols), f32), V((seq, cols), bf16),
             V((3, seq + PAD, cols), f32), V((seq, cols), f32), V((seq, cols), f32), V((8, cols), f32),
             V((seq, cols), bf16), V((seq, cols), f32),
-            dma((5,)), dma((near,)), dma((near,)), dma((near,)), dma((near,)),
+            dma((5,)), dma((near,)), dma((near,)), dma((2 * near,)), dma((2 * near,)),
             dma((peers * near,)), dma((peers * near,)), dma((near,)), dma((near,)), dma((near,)), dma((near,)),
-            dma((near,)), dma((near,)), dma((near,)), dma((near,)), dma((near,)), dma((near,)),
+            dma((2 * near,)), dma((2 * near,)), dma((near,)), dma((near,)), dma((near,)), dma((near,)),
         ],
         compiler_params=pltpu.CompilerParams(
             collective_id=0, has_side_effects=True, vmem_limit_bytes=56 * 1024 * 1024

time: 104 us -> 94.6 us (0.910)
  Pallas kernels: 90.1 us -> 81.6 us
    pallas_call x1, Pallas kernels: 90.1 us -> 81.6 us  [body(): pl.pallas_call(mega, out_shape=(S((3, tokens, width), bf16), S((16, width...]
where the time goes in v3:
time: 94.6 us; the launch traced here: 94.1 us
  Pallas kernels  81.6 us (86%)
  local copies, waits for them, and re-layouts  11.9 us (13%)
    pallas_call x1, Pallas kernels, body(): pl.pallas_call(mega, out_shape=(S((3, tokens, width), bf16), S((16, width...  81.6 us
    unnamed x7, local copies, waits for them, and re-layouts  9.8 us

profile of v3, /device:TPU:0, one launch (start us, length us, event | category | flops | bytes accessed | tf_op | source)
XLA Modules:
  0.0 94.1 jit_solution(12046948510445334198)
XLA Ops:
  0.6 0.0 copy-start
  0.7 0.8 copy-done
  1.4 0.6 reshape.18.taps
  2.1 81.6 %shard_map.127 = (bf16[3,128,1024]{2,1,0:T(8,128)(2,1)}, f32[16,1024]{1,0:T(8,128)}, f32[1,256]{1,0:T(1,128)}, f32[16,256]{1,0:T(8,128)}, f32[16,256]{1,0:T(8,128)}, /*index=5*/f32[1024,512]{1,0:T(8,128)}) custom-call(bf16[3,128,1024]{2,1,0:T(8,128)(2,1)} %bitcast.10, bf16[1024,512]{1,0:T(8,128)(2,1)} %w.1, bf16[128,512]{1,0:T(8,128)(2,1)} %gm.1, ...), custom_call_target="tpu_custom_call" | custom-call | tf_op jit(solution)/shard_map/pallas_call | solution.py:546
  83.7 1.5 %reshape.19 = f32[3,3,1024]{2,1,0:T(4,128)} reshape(f32[9,1024]{1,0:T(8,128)} %bitcast.11) | data formatting | bytes 73728 | tf_op jit(solution)/shard_map/reshape | solution.py:577
  85.1 2.1 %copy.19 = bf16[128,3,1024]{2,0,1:T(8,128)(2,1)} copy(bf16[128,3,1024]{2,0,1:T(8,128)(2,1)} %bitcast.9) | data formatting | bytes 1572864
  87.2 1.2 %copy.20 = f32[256]{0:T(256)} copy(f32[256]{0:T(256)} %bitcast.17) | data formatting | bytes 2048
  88.4 1.3 %copy.21 = f32[256,16]{0,1:T(8,128)} copy(f32[256,16]{0,1:T(8,128)} %bitcast.15) | data formatting | bytes 32768
  89.7 1.3 %copy.22 = f32[256,16]{0,1:T(8,128)} copy(f32[256,16]{0,1:T(8,128)} %bitcast.14) | data formatting | bytes 32768
  91.1 3.1 %copy.23 = f32[1024,512]{1,0:T(8,128)} copy(f32[1024,512]{1,0:T(8,128)} %get-tuple-element.29) | data formatting | bytes 4194304
  (1 shorter events, 0.0 us)
Async XLA Ops:
  0.6 0.8 copy-start

commit v4 on v3

--- a/solution.py
+++ b/solution.py
@@ -199,8 +199,8 @@
 
 def mega(
     proj, w, gm, taps, gain, res, rate, tab,
-    o_proj, o_short, o_skip, o_res, o_rate, o_weight,
-    pbuf, wbuf, gbuf, mbuf, gp, short_own,
+    o_proj, o_short, o_skip, o_res, o_rate, mbuf, o_gm,
+    pbuf, wbuf, gbuf, gp, short_own,
     wh, wl, th, tl, pq, ab, de, sp_h, sp_l, x_h, x_l,
     pf, qkv, gated, gmix, gout, mix, filt, gy, gf,
     loc, s_p, r_p, s_g, r_g, s_gf, r_gf, s_w, r_w, s_wf, r_wf, s_m, r_m, s_o, r_o, s_s, r_s,
@@ -306,13 +306,6 @@
         zp = ring(z, d)
         c_p[d] = remote(proj.at[:, :, span(zp, cols)], pbuf.at[:, span(z, tokens), :], s_p.at[d - 1], r_p.at[d - 1], ctx=zp)
         c_p[d].start()
-    for d in order:
-        zp = ring(z, d)
-        c_w[d] = remote(
-            w.at[pl.ds(pl.multiple_of(zp * cols + g * half, half), half), :],
-            wbuf.at[z, span(g, half), :], s_w.at[d - 1], r_w.at[d - 1], ctx=zp,
-        )
-        c_w[d].start()
     groups_of = seq // FINE
     at = [0]
     for n in (groups_of, groups_of, FINE, FINE, groups_of, groups_of, FINE, FINE):
@@ -383,6 +376,15 @@
         gmix[i, seq : seq + PAD] = jnp.zeros((PAD, cols), f32)
     gain_row = gain[...]
 
+    for d in order:
+        c_p[d].wait_send()
+    for d in order:
+        zp = ring(z, d)
+        c_w[d] = remote(
+            w.at[pl.ds(pl.multiple_of(zp * cols + g * half, half), half), :],
+            wbuf.at[z, span(g, half), :], s_w.at[d - 1], r_w.at[d - 1], ctx=zp,
+        )
+        c_w[d].start()
     local[0].wait()
     for d in order:
         c_p[d].wait_recv()
@@ -420,6 +422,8 @@
     for d in order:
         c_wf[d].wait_recv()
 
+    keep = pltpu.make_async_copy(gbuf.at[z], o_gm, loc.at[3])
+    keep.start()
     for r in range(0, seq, block):
         rows = slice(r, r + block)
         total = jnp.zeros((block, cols), f32)
@@ -433,6 +437,23 @@
         go = gout[rows]
         gy[rows] = (go * qkv[0, rows]).astype(bf16)
         gmix[0, rows] = go * mix[rows]
+    c_o, c_s, own = {}, {}, {}
+
+    def send_gradient(i):
+        for r in range(0, seq, ROWS):
+            total = jnp.zeros((ROWS, cols), f32)
+            for j in range(SHORT):
+                total = total + taps[3 * j + i : 3 * j + i + 1] * gmix[i, r + j : r + j + ROWS]
+            gp[i, r : r + ROWS] = total.astype(bf16)
+        for d in order:
+            zp = ring(z, d)
+            n = i * (peers - 1) + d - 1
+            c_o[i, d] = remote(gp.at[i, span(zp, tokens), :], o_proj.at[i, :, span(z, cols)], s_o.at[n], r_o.at[n], ctx=zp)
+            c_o[i, d].start()
+        own[i] = pltpu.make_async_copy(gp.at[i, span(z, tokens), :], o_proj.at[i, :, span(z, cols)], loc.at[5 + i])
+        own[i].start()
+
+    send_gradient(0)
     spectrum(de, gy)
     product(pq, de, True)
     line_step(1, mixed_block, s_m, r_m)
@@ -441,19 +462,8 @@
         gg = (inverse(r, block) + gain_row * gy[rows].astype(f32)).astype(bf16).astype(f32)
         gmix[1, rows] = gg * qkv[2, rows]
         gmix[2, rows] = gg * qkv[1, rows]
-    for r in range(0, seq, ROWS):
-        for i in range(3):
-            total = jnp.zeros((ROWS, cols), f32)
-            for j in range(SHORT):
-                total = total + taps[3 * j + i : 3 * j + i + 1] * gmix[i, r + j : r + j + ROWS]
-            gp[i, r : r + ROWS] = total.astype(bf16)
-    c_o, c_s = {}, {}
-    for d in order:
-        zp = ring(z, d)
-        c_o[d] = remote(gp.at[:, span(zp, tokens), :], o_proj.at[:, :, span(z, cols)], s_o.at[d - 1], r_o.at[d - 1], ctx=zp)
-        c_o[d].start()
-    own = pltpu.make_async_copy(gp.at[:, span(z, tokens), :], o_proj.at[:, :, span(z, cols)], loc.at[3])
-    own.start()
+    for i in (1, 2):
+        send_gradient(i)
 
     def fold(x):
         return jnp.sum(x.reshape(ROWS // 8, 8, cols), axis=0)
@@ -500,26 +510,32 @@
 
     lax.fori_loop(0, order_n, moments, 0)
 
-    def weight(zs):
-        o_weight[span(zs, cols), :] = dot(mbuf[zs], gbuf[z]) * (1.0 / norm)
-
-    weight(z)
     line_step(2, mixed_block, s_m, r_m)
-    for d in hops:
-        weight(ring(z, d))
+    keep.wait()
     for group in (c_o, c_s):
-        for d in order:
-            group[d].wait_recv()
-    own.wait()
+        for key in group:
+            group[key].wait_recv()
+    for i in own:
+        own[i].wait()
     own_short.wait()
     line_end(gm_block, s_g, r_g)
     line_end(mixed_block, s_m, r_m)
     for zs in range(peers):
         for where in range(3):
             gm_out(zs, where).wait_send()
-    for group in (c_p, c_w, c_wf, c_o, c_s):
+    for group in (c_w, c_wf, c_o, c_s):
         for key in group:
             group[key].wait_send()
+
+
+def finish(mixed, gm, rows, short, skip, res, rate, o_weight, o_rows, o_short, o_skip, o_res, o_rate):
+    o_weight[...] = dot(mixed[0], gm[...]) * (1.0 / math.sqrt(gm.shape[0]))
+    o_rows[...] = rows[...]
+    for j in range(SHORT):
+        o_short[j] = short[3 * j : 3 * j + 3]
+    o_skip[...] = skip[...]
+    o_res[...] = res[...]
+    o_rate[...] = rate[...]
 
 
 def body(projections, short_taps, residues, decay_rates, skip_gain, grad_mixed, out_weight):
@@ -547,22 +563,23 @@
         mega,
         out_shape=(
             S((3, tokens, width), bf16), S((16, width), f32), S((1, cols), f32),
-            S((order, cols), f32), S((order, cols), f32), S((width, wide), f32),
+            S((order, cols), f32), S((order, cols), f32),
+            S((peers, cols, seq), bf16), S((seq, wide), bf16),
         ),
         in_specs=[any_, any_, any_] + [vmem] * 5,
-        out_specs=[vmem] * 6,
+        out_specs=[vmem] * 7,
         scratch_shapes=[
             V((3, seq, cols), bf16), V((peers, cols, wide), bf16), V((peers, seq, wide), bf16),
-            V((peers, cols, seq), bf16), V((3, seq, cols), bf16), V((16, cols), f32),
+            V((3, seq, cols), bf16), V((16, cols), f32),
             V((2 * seq, seq), bf16), V((2 * seq, seq), bf16), V((seq, 2 * seq), bf16), V((seq, 2 * seq), bf16),
             V((2 * seq, cols), f32), V((2 * seq, cols), f32), V((2 * seq, cols), f32),
             V((2 * seq, cols), bf16), V((2 * seq, cols), bf16), V((seq, cols), bf16), V((seq, cols), bf16),
             V((3, PAD + seq, cols), f32), V((3, seq, cols), f32), V((seq, cols), bf16),
             V((3, seq + PAD, cols), f32), V((seq, cols), f32), V((seq, cols), f32), V((8, cols), f32),
             V((seq, cols), bf16), V((seq, cols), f32),
-            dma((5,)), dma((near,)), dma((near,)), dma((2 * near,)), dma((2 * near,)),
+            dma((8,)), dma((near,)), dma((near,)), dma((2 * near,)), dma((2 * near,)),
             dma((peers * near,)), dma((peers * near,)), dma((near,)), dma((near,)), dma((near,)), dma((near,)),
-            dma((2 * near,)), dma((2 * near,)), dma((near,)), dma((near,)), dma((near,)), dma((near,)),
+            dma((2 * near,)), dma((2 * near,)), dma((3 * near,)), dma((3 * near,)), dma((near,)), dma((near,)),
         ],
         compiler_params=pltpu.CompilerParams(
             collective_id=0, has_side_effects=True, vmem_limit_bytes=56 * 1024 * 1024
@@ -571,11 +588,33 @@
         projections.transpose(1, 0, 2), out_weight, grad_mixed, taps, skip_gain[None],
         residues.T, decay_rates.T, tables,
     )
-    grad_proj, short, skip, grad_res, grad_rate, grad_weight = outs
+    proj_rows, short, skip, grad_res, grad_rate, mixed, gm_own = outs
+
+    def whole(shape):
+        return pl.BlockSpec(shape, lambda i: (0,) * len(shape))
+
+    rows_spec = pl.BlockSpec((3, tokens, cols), lambda i: (0, 0, i))
+    grad_weight, grad_proj, grad_short, grad_skip, grad_res, grad_rate = pl.pallas_call(
+        finish,
+        grid=(peers,),
+        out_shape=(
+            S((width, wide), f32), S((3, tokens, width), bf16), S((SHORT, 3, width), f32),
+            S((1, cols), f32), S((order, cols), f32), S((order, cols), f32),
+        ),
+        in_specs=[
+            pl.BlockSpec((1, cols, seq), lambda i: (i, 0, 0)), whole((seq, wide)), rows_spec,
+            pl.BlockSpec((16, cols), lambda i: (0, i)), whole((1, cols)), whole((order, cols)), whole((order, cols)),
+        ],
+        out_specs=[
+            pl.BlockSpec((cols, wide), lambda i: (i, 0)), rows_spec,
+            pl.BlockSpec((SHORT, 3, cols), lambda i: (0, 0, i)),
+            whole((1, cols)), whole((order, cols)), whole((order, cols)),
+        ],
+    )(mixed, gm_own, proj_rows, short, skip, grad_res, grad_rate)
     return (
         grad_proj.transpose(1, 0, 2),
-        short[: SHORT * 3].reshape(SHORT, 3, width),
-        skip[0],
+        grad_short,
+        grad_skip[0],
         grad_res.T,
         grad_rate.T,
         grad_weight,

time: 94.6 us -> 84.3 us (0.89)
  local copies, waits for them, and re-layouts: 11.9 us -> 1.41 us
    unnamed x7 -> x2, local copies, waits for them, and re-layouts: 9.8 us -> 0.79 us
    pallas_call x0 -> x1, Pallas kernels: none -> 4.74 us  [body(): pl.pallas_call(finish, grid=(peers,), out_shape=(S((width, wide), f32), S...]
    pallas_call x1, Pallas kernels: 81.6 us -> 77.2 us  [body(): pl.pallas_call(mega, out_shape=(S((3, tokens, width), bf16), S((16, width...]
    reshape x1 -> x0, local copies, waits for them, and re-layouts: 1.48 us -> none  [body(): short[:SHORT * 3].reshape(SHORT, 3, width)]
where the time goes in v4:
time: 84.3 us; the launch traced here: 84 us
  Pallas kernels  82 us (97%)
  local copies, waits for them, and re-layouts  1.41 us (2%)
    pallas_call x1, Pallas kernels, body(): pl.pallas_call(mega, out_shape=(S((3, tokens, width), bf16), S((16, width...  77.2 us
    pallas_call x1, Pallas kernels, body(): pl.pallas_call(finish, grid=(peers,), out_shape=(S((width, wide), f32), S...  4.74 us

profile of v4, /device:TPU:0, one launch (start us, length us, event | category | flops | bytes accessed | tf_op | source)
XLA Modules:
  0.0 84.0 jit_solution(15283585805560111234)
XLA Ops:
  0.6 0.0 copy-start
  0.7 0.8 copy-done
  1.4 0.6 reshape.15.taps
  2.1 77.2 %shard_map.127 = (bf16[3,128,1024]{2,1,0:T(8,128)(2,1)}, f32[16,1024]{1,0:T(8,128)}, f32[1,256]{1,0:T(1,128)}, f32[16,256]{1,0:T(8,128)}, f32[16,256]{1,0:T(8,12...) custom-call(bf16[3,128,1024]{2,1,0:T(8,128)(2,1)} %bitcast.8, bf16[1024,512]{1,0:T(8,128)(2,1)} %w.1, ...), custom_call_target="tpu_custom_call" | custom-call | tf_op jit(solution)/shard_map/pallas_call | solution.py:562
  79.3 4.7 %shard_map.128 = (f32[1024,512]{1,0:T(8,128)}, bf16[3,128,1024]{2,1,0:T(8,128)(2,1)}, f32[3,3,1024]{2,1,0:T(4,128)}, f32[1,256]{1,0:T(1,128)}, f32[16,256]{1,0:T(8,128)}, /*index=5*/f32[16,256]{1,0:T(8,128)}) custom-call(bf16[4,256,512]{2,1,0:T(8,128)(2,1)} %get-tuple-element.19.mixed, bf16[512,512]{1,0:T(8,128)(2,1)} %get-tuple-element.20.gm, ...), custom_call_target="tpu_custom_call" | custom-call | tf_op jit(solution)/shard_map/pallas_call | solution.py:597
  (1 shorter events, 0.0 us)
Async XLA Ops:
  0.6 0.8 copy-start
